TPU v7x, 32 devices: a whole 2x2x4 slice. The times are simulated.
32 devices in a mesh: grp: 4 (over y, x), seq: 8 (over z, core).
Axes of the slice: x: 2, y: 2, z: 4, core: 2. Of those that a mesh axis runs over, the one named last changes fastest.
Arguments:
- owned_patches: bfloat16 [4, 1024, 1152], P('grp', 'seq'), may hold values from -6 to 6
- send_rows: int32 [4, 8, 128], P('grp', 'seq'), may hold values from 0 to 127, each once within a row
- receive_slot: int32 [4, 8, 128], P('grp', 'seq'), may hold values from 0 to 127, each once within a row
- segment_ids: int32 [4, 1024], P('grp', 'seq'), may hold values from 0 to 15, never falling along the last dimension, each value on 1 to 640 neighbouring positions
- class_label: int32 [4, 16], P('grp'), may hold values from 0 to 999
- drop_mask: int32 [4, 16], P('grp'), may hold values 0 or 1
- class_table: bfloat16 [1001, 1152], replicated, may hold values from -6 to 6
- modulation_weight: bfloat16 [1152, 3456], replicated, may hold values from -0.1875 to 0.1875
- attention_in: bfloat16 [1152, 1728], replicated, may hold values from -0.1875 to 0.1875
- attention_out: bfloat16 [576, 1152], replicated, may hold values from -0.25 to 0.25
- cotangent: bfloat16 [4, 1024, 1152], P('grp', 'seq'), may hold values from -6 to 6
Outputs:
- layer_output: bfloat16 [4, 1024, 1152], P('grp', 'seq')
- owner_gradient: bfloat16 [4, 1024, 1152], P('grp', 'seq')
- gradient_in: bfloat16 [1152, 1728], replicated
- gradient_out: bfloat16 [576, 1152], replicated
Inputs may be any that keep to these rules, and one draw needn't show every extreme that they name: `send_rows`: for owner shard s of a group, entries 16 * d to 16 * d + 15 name, in slot order, the local rows that go to packed shard d; every local row once. `receive_slot`: packed row r of packed shard d takes slot c of what owner shard s sends to d, where the entry is 16 * s + c; every slot once. `segment_ids`: never falling along a group's tokens; every image has 1 to 640 tokens, one exactly 640.
All inputs are finite; a program needn't handle non-finite values. No bound on the sum of `drop_mask` on one device may be relied on, other than what follows from the above.
Results may differ from a plain program's by a relative error of at most 0.015.
Values may be sent and summed in bfloat16 or wider, within the bound.
A program may use at most 128 MiB of HBM per device.

v0:
```python
import math

import jax
import jax.numpy as jnp
from jax import lax
from jax.sharding import PartitionSpec as P

HEADS = 8
CLASSES = 1000


EPSILON = 1e-06


def normalize(values):
    center = values - jnp.mean(values, axis=-1, keepdims=True)
    spread = jnp.mean(center * center, axis=-1, keepdims=True)
    inverse_spread = lax.rsqrt(spread + EPSILON)
    return (center * inverse_spread, inverse_spread)


def exponent(query_heads, key_heads, image_query, image_keys, factor):
    logits = (
        jnp.einsum("qhe,khe->qhk", query_heads, key_heads, preferred_element_type=jnp.float32)
        * factor
    )
    joined = (image_query[:, None] == image_keys[None, :])[:, None, :]
    return jnp.exp(jnp.where(joined, logits, -jnp.inf))


def shards(
    owned_patches,
    send_rows,
    receive_slot,
    segment_ids,
    class_label,
    drop_mask,
    class_table,
    modulation_weight,
    attention_in,
    attention_out,
    cotangent,
):
    shard_count = lax.axis_size("seq")
    tokens = owned_patches.shape[1]
    model_width = owned_patches.shape[2]
    inner_width = attention_out.shape[0]
    head_width = inner_width // HEADS
    factor = head_width ** (-0.5)
    outgoing = jnp.take(owned_patches[0], send_rows[0, 0], axis=0)
    incoming = lax.all_to_all(outgoing, "seq", split_axis=0, concat_axis=0, tiled=True)
    packed = jnp.take(incoming, receive_slot[0, 0], axis=0)
    chosen = jnp.where(drop_mask[0] == 1, CLASSES, class_label[0])
    condition = jnp.take(class_table, chosen, axis=0)
    activated = jax.nn.silu(condition.astype(jnp.float32)).astype(jnp.bfloat16)
    modulation = jnp.dot(activated, modulation_weight, preferred_element_type=jnp.float32)
    local_images = segment_ids[0]
    image_count = class_label.shape[1]
    one_hot = (local_images[:, None] == jnp.arange(image_count, dtype=jnp.int32)[None, :]).astype(
        jnp.float32
    )
    per_token = jnp.dot(
        one_hot, modulation, precision=lax.Precision.HIGHEST, preferred_element_type=jnp.float32
    )
    shift_rows = per_token[:, :model_width]
    scale_rows = per_token[:, model_width : 2 * model_width]
    gate_rows = per_token[:, 2 * model_width :]
    row_values = packed.astype(jnp.float32)
    normed, inverse_spread = normalize(row_values)
    hidden = (normed * (1.0 + scale_rows) + shift_rows).astype(jnp.bfloat16)
    projected_in = jnp.dot(hidden, attention_in, preferred_element_type=jnp.float32).astype(
        jnp.bfloat16
    )
    queries = projected_in[:, :inner_width]
    key_value = projected_in[:, inner_width:]
    all_key_value, all_images = (
        lax.all_gather(key_value, "seq", axis=0, tiled=True),
        lax.all_gather(local_images, "seq", axis=0, tiled=True),
    )
    total_rows = all_key_value.shape[0]
    block_rows = math.gcd(total_rows, 512)
    block_count = total_rows // block_rows
    query_heads = queries.reshape(tokens, HEADS, head_width)

    def key_block(block_index):
        first_row = block_index * block_rows
        block_pair = lax.dynamic_slice_in_dim(all_key_value, first_row, block_rows, 0)
        block_images = lax.dynamic_slice_in_dim(all_images, first_row, block_rows, 0)
        key_heads = block_pair[:, :inner_width].reshape(block_rows, HEADS, head_width)
        value_heads = block_pair[:, inner_width:].reshape(block_rows, HEADS, head_width)
        return (key_heads, value_heads, block_images)

    def forward_step(block_index, carried):
        weighted, totals = carried
        key_heads, value_heads, block_images = key_block(block_index)
        powers = exponent(query_heads, key_heads, local_images, block_images, factor)
        totals = totals + jnp.sum(powers, axis=-1)
        weighted = weighted + jnp.einsum(
            "qhk,khe->qhe",
            powers.astype(jnp.bfloat16),
            value_heads,
            preferred_element_type=jnp.float32,
        )
        return (weighted, totals)

    start_state = (
        jnp.zeros((tokens, HEADS, head_width), jnp.float32),
        jnp.zeros((tokens, HEADS), jnp.float32),
    )
    weighted, totals = lax.fori_loop(0, block_count, forward_step, start_state)
    attended = (weighted / totals[:, :, None]).reshape(tokens, inner_width).astype(jnp.bfloat16)
    projected = jnp.dot(attended, attention_out, preferred_element_type=jnp.float32)
    layer_output = (row_values + gate_rows * projected).astype(jnp.bfloat16)
    contract_rows = (((0,), (0,)), ((), ()))
    contract_last = (((1,), (1,)), ((), ()))
    upstream = cotangent[0].astype(jnp.float32)
    branch = (gate_rows * upstream).astype(jnp.bfloat16)
    out_weight_term = lax.dot_general(
        attended, branch, contract_rows, preferred_element_type=jnp.float32
    )
    attended_cotangent = lax.dot_general(
        branch, attention_out, contract_last, preferred_element_type=jnp.float32
    ).astype(jnp.bfloat16)
    cotangent_heads = attended_cotangent.reshape(tokens, HEADS, head_width)
    attended_heads = attended.reshape(tokens, HEADS, head_width)
    delta_rows = jnp.sum(
        cotangent_heads.astype(jnp.float32) * attended_heads.astype(jnp.float32), axis=-1
    )

    def query_step(block_index, carried):
        key_heads, value_heads, block_images = key_block(block_index)
        weights = (
            exponent(query_heads, key_heads, local_images, block_images, factor)
            / totals[:, :, None]
        )
        weight_cotangent = jnp.einsum(
            "qhe,khe->qhk", cotangent_heads, value_heads, preferred_element_type=jnp.float32
        )
        score_cotangent = (weights * (weight_cotangent - delta_rows[:, :, None])).astype(
            jnp.bfloat16
        )
        return carried + jnp.einsum(
            "qhk,khe->qhe", score_cotangent, key_heads, preferred_element_type=jnp.float32
        )

    query_sum = lax.fori_loop(
        0, block_count, query_step, jnp.zeros((tokens, HEADS, head_width), jnp.float32)
    )
    all_totals, all_delta = (
        lax.all_gather(totals, "seq", axis=0, tiled=True),
        lax.all_gather(delta_rows, "seq", axis=0, tiled=True),
    )
    local_keys = key_value[:, :inner_width].reshape(tokens, HEADS, head_width)
    local_values = key_value[:, inner_width:].reshape(tokens, HEADS, head_width)
    query_pair = jnp.concatenate([queries, attended_cotangent], axis=1)
    piece_rows = lax.all_gather(query_pair, "seq", axis=0, tiled=True)
    piece_images = lax.all_gather(local_images, "seq", axis=0, tiled=True)
    row_count = piece_rows.shape[0]
    piece_queries = piece_rows[:, :inner_width].reshape(row_count, HEADS, head_width)
    piece_cotangent = piece_rows[:, inner_width:].reshape(row_count, HEADS, head_width)
    weights = (
        exponent(piece_queries, local_keys, piece_images, local_images, factor)
        / all_totals[:, :, None]
    )
    weight_cotangent = jnp.einsum(
        "qhe,khe->qhk", piece_cotangent, local_values, preferred_element_type=jnp.float32
    )
    score_cotangent = (weights * (weight_cotangent - all_delta[:, :, None])).astype(jnp.bfloat16)
    key_part = jnp.einsum(
        "qhk,qhe->khe", score_cotangent, piece_queries, preferred_element_type=jnp.float32
    )
    value_part = jnp.einsum(
        "qhk,qhe->khe",
        weights.astype(jnp.bfloat16),
        piece_cotangent,
        preferred_element_type=jnp.float32,
    )
    key_sum = key_part.reshape(tokens, inner_width)
    value_sum = value_part.reshape(tokens, inner_width)
    input_cotangent = jnp.concatenate(
        [
            (query_sum * factor).reshape(tokens, inner_width).astype(jnp.bfloat16),
            (key_sum * factor).astype(jnp.bfloat16),
            value_sum.astype(jnp.bfloat16),
        ],
        axis=1,
    )
    in_weight_term = lax.dot_general(
        hidden, input_cotangent, contract_rows, preferred_element_type=jnp.float32
    )
    in_summed, out_summed = lax.psum((in_weight_term, out_weight_term), ("grp", "seq"))
    norm_factor = (lax.axis_size("grp") * shard_count * tokens) ** (-0.5)
    hidden_cotangent = lax.dot_general(
        input_cotangent, attention_in, contract_last, preferred_element_type=jnp.float32
    )
    scaled_cot = hidden_cotangent * (1.0 + scale_rows)
    packed_cotangent = upstream + inverse_spread * (
        scaled_cot
        - jnp.mean(scaled_cot, axis=-1, keepdims=True)
        - normed * jnp.mean(scaled_cot * normed, axis=-1, keepdims=True)
    )
    packed_low = packed_cotangent.astype(jnp.bfloat16)
    back_order = jnp.zeros_like(packed_low).at[receive_slot[0, 0]].set(packed_low)
    returned = lax.all_to_all(back_order, "seq", split_axis=0, concat_axis=0, tiled=True)
    owner_gradient = jnp.zeros_like(returned).at[send_rows[0, 0]].set(returned)
    return (
        layer_output[None],
        owner_gradient[None],
        (in_summed * norm_factor).astype(jnp.bfloat16),
        (out_summed * norm_factor).astype(jnp.bfloat16),
    )


def solution(mesh):
    return jax.shard_map(
        shards,
        mesh=mesh,
        in_specs=(
            P("grp", "seq", None),
            P("grp", "seq", None),
            P("grp", "seq", None),
            P("grp", "seq"),
            P("grp", None),
            P("grp", None),
            P(),
            P(),
            P(),
            P(),
            P("grp", "seq", None),
        ),
        out_specs=(P("grp", "seq", None), P("grp", "seq", None), P(), P()),
        check_vma=False,
    )
```

profile of v0, /device:TPU:0, one launch (start us, length us, event | category | flops | bytes accessed | tf_op | source)
XLA Modules:
  0.0 364.7 jit_solution(1085323772350284070)
XLA Ops:
  8.7 2.1 gather_fusion.1
  11.6 6.4 %all-to-all-start = ((bf16[8,16,1152]{2,1,0:T(8,128)(2,1)}), bf16[8,16,1152]{2,1,0:T(8,128)(2,1)S(1)}, u32[]{:S(2)}, u32[]{:S(2)}) async-start(bf16[8,16,1152]{2,1,0:T(8,128)(2,1)} %bitcast.3), calls=%async_computation | async-start | bytes 589824 | tf_op jit(solution)/shard_map/all_to_all | solution.py:51
  18.7 4.5 %fusion.72 = f32[16,3456]{1,0:T(8,128)S(1)} fusion(bf16[1152,3456]{1,0:T(8,128)(2,1)} %param.24, bf16[16,1152]{1,0:T(8,128)(2,1)S(1)} %gather_fusion, pred[16]{0:T(512)(128)(4,1)S(1)} %compare_and_fusion.2), kind=kOutput, calls=%fused_computation.105 | convolution fusion | flops 127531008 | bytes 8220688 | tf_op jit(solution)/shard_map/dot_general | solution.py:56
  24.2 4.2 %all-to-all-done = bf16[8,16,1152]{2,1,0:T(8,128)(2,1)S(1)} async-done(((bf16[8,16,1152]{2,1,0:T(8,128)(2,1)}), bf16[8,16,1152]{2,1,0:T(8,128)(2,1)S(1)}, u32[]{:S(2)}, u32[]{:S(2)}) %all-to-all-start) | async-done | bytes 294944 | tf_op jit(solution)/shard_map/all_to_all | solution.py:51
  30.1 3.4 convolution_convert_fusion
  34.4 1.9 convolution_convert_fusion.1
  37.2 9.8 %all-gather = s32[1,1024]{1,0:T(1,128)S(1)} all-gather(s32[1,128]{1,0:T(1,128)S(1)} %copy-done.19), channel_id=2, replica_groups=mesh['grp'=4,'seq'=8] {'seq'}, dimensions={1}, use_global_device_ids=true | all-gather | bytes 4608 | tf_op jit(solution)/shard_map/all_gather | solution.py:78
  49.5 16.6 %all-gather.4.cloned.1.call-done = bf16[1024,1152]{0,1:T(8,128)(2,1)} async-done(((bf16[128,1152]{0,1:T(8,128)(2,1)}), bf16[1024,1152]{0,1:T(8,128)(2,1)}) %all-gather.4.cloned.1.call-update) | async-done | bytes 2359312 | tf_op jit(solution)/shard_map/all_gather | solution.py:77
  66.1 5.9 %while.30 = (s32[]{:T(128)}, f32[128,8,72]{0,2,1:T(8,128)S(1)}, f32[128,8]{0,1:T(8,128)S(1)}, bf16[1024,1152]{0,1:T(8,128)(2,1)}, s32[1,128]{1,0:T(1,128)S(1)}, ...) while((s32[]{:T(128)}, f32[128,8,72]{0,2,1:T(8,128)S(1)}, ...), condition=%wide.region_4.6_spmd.clone, body=%wide.region_2.5_spmd.clone.sunk | while | flops 154354688 | bytes 8690382 | solution.py:110
  72.0 14.3 %all_gather.19 = f32[1024,8]{0,1:T(8,128)S(1)} all-gather(f32[128,8]{0,1:T(8,128)S(1)} %get-tuple-element.554), channel_id=1, replica_groups=mesh['grp'=4,'seq'=8] {'seq'}, dimensions={0}, use_global_device_ids=true | all-gather | bytes 36864 | tf_op jit(solution)/shard_map/all_gather | solution.py:150
  86.4 14.5 %all_gather.20 = f32[1024,8]{0,1:T(8,128)S(1)} all-gather(f32[128,8]{0,1:T(8,128)S(1)} %get-tuple-element.556), channel_id=1, replica_groups=mesh['grp'=4,'seq'=8] {'seq'}, dimensions={0}, use_global_device_ids=true | all-gather | bytes 36864 | tf_op jit(solution)/shard_map/all_gather | solution.py:151
  100.9 12.2 %while.31 = (s32[]{:T(128)}, f32[128,8,72]{0,2,1:T(8,128)S(1)}, bf16[1024,1152]{0,1:T(8,128)(2,1)}, s32[1,128]{1,0:T(1,128)S(1)}, s32[1024]{0:T(1024)S(1)}, /*in...) while((s32[]{:T(128)}, f32[128,8,72]{0,2,1:T(8,128)S(1)}, ...), condition=%wide.region_7.9_spmd.clone, body=%wide.region_6.8_spmd.clone.sunk | while | flops 229851136 | bytes 9943801 | solution.py:146
  101.1 1.4 fusion.140
  102.5 1.7 fusion.141
  104.2 2.7 fusion.142
  107.2 1.4 fusion.140
  108.5 1.7 fusion.141
  110.3 2.7 fusion.142
  113.1 3.1 fusion.86
  116.3 1.9 fusion.91
  118.2 1.3 fusion.31
  121.5 4.5 %fusion.39 = bf16[8,72,128]{2,1,0:T(8,128)(2,1)} fusion(bf16[1024,8,72]{0,2,1:T(8,128)(2,1)S(1)} %bitcast.192, f32[1024,8,128]{0,2,1:T(8,128)} %copy-done.2, bf16[128,8,72]{0,2,1:T(8,128)(2,1)} %bitcast.205, bf16[1024,8,72]{0,2,1:T(8,128)(2,1)S(1)} %bitcast.190, f32[1024,8]{0,1:T(8,128)S(1)} %all_gather.20), kind=kOutput, calls=%fused_computation.58 | convolution fusion | flops 305283072 | bytes 6881280 | tf_op jit(solution)/shard_map/qhk,qhe->khe/dot_general | solution.py:169
  126.0 5.2 %fusion.63 = f32[1152,1728]{0,1:T(8,128)} fusion(bf16[128,1152]{1,0:T(8,128)(2,1)S(1)} %copy-done.9, bf16[128,576]{0,1:T(8,128)(2,1)S(1)} %bitcast.199, bf16[128,576]{0,1:T(8,128)(2,1)} %bitcast.203, bf16[128,576]{0,1:T(8,128)(2,1)S(1)} %bitcast.201), kind=kOutput, calls=%fused_computation.93 | convolution fusion | flops 510935040 | bytes 8699904 | tf_op jit(solution)/shard_map/dot_general | solution.py:188
  131.2 1.4 copy-done.4
  132.7 3.1 fusion.89
  135.9 2.1 scatter_custom_fusion
  137.9 4.4 %all-to-all-start.1 = ((bf16[8,16,1152]{2,1,0:T(8,128)(2,1)}), bf16[8,16,1152]{2,1,0:T(8,128)(2,1)S(1)}, u32[]{:S(2)}, u32[]{:S(2)}) async-start(bf16[8,16,1152]{2,1,0:T(8,128)(2,1)} %bitcast.31), calls=%async_computation.1 | async-start | bytes 589824 | tf_op jit(solution)/shard_map/all_to_all | solution.py:204
  142.3 2.5 fusion.34
  144.8 10.5 %all-to-all-done.1 = bf16[8,16,1152]{2,1,0:T(8,128)(2,1)S(1)} async-done(((bf16[8,16,1152]{2,1,0:T(8,128)(2,1)}), bf16[8,16,1152]{2,1,0:T(8,128)(2,1)S(1)}, u32[]{:S(2)}, u32[]{:S(2)}) %all-to-all-start.1) | async-done | bytes 294944 | tf_op jit(solution)/shard_map/all_to_all | solution.py:204
  155.4 1.8 scatter_custom_fusion.1
  157.2 193.7 %all-reduce.3.cloned.1.call-done = (f32[1152,1728]{0,1:T(8,128)}, f32[576,1152]{1,0:T(8,128)}) async-done(((f32[1152,1728]{0,1:T(8,128)}, f32[576,1152]{1,0:T(8,128)}), (f32[1152,1728]{0,1:T(8,128)}, f32[576,1152]{1,0:T(8,128)})) %all-reduce.3.cloned.1.call-update) | async-done | bytes 10616848 | tf_op jit(solution)/shard_map/psum | solution.py:191
  350.9 6.0 %multiply_convert_fusion = bf16[1152,1728]{0,1:T(8,128)(2,1)} fusion(f32[1152,1728]{0,1:T(8,128)} %get-tuple-element.384), kind=kLoop, calls=%fused_computation.40 | loop fusion | flops 3981312 | bytes 11943936 | tf_op jit(solution)/shard_map/convert_element_type | solution.py:209
  (106 shorter events, 19.4 us)
Async XLA Ops:
  7.2 11.0 %copy-start = (bf16[1001,1152]{1,0:T(8,128)(2,1)S(1)}, bf16[1001,1152]{1,0:T(8,128)(2,1)}, u32[]{:S(2)}) copy-start(bf16[1001,1152]{1,0:T(8,128)(2,1)} %param.23) | copy-start | bytes 6918916
  7.2 10.9 %copy-start.21 = (s32[1,16]{1,0:T(1,128)S(1)}, s32[1,16]{1,0:T(1,128)}, u32[]{:S(2)}) copy-start(s32[1,16]{1,0:T(1,128)} %param.22) | copy-start | bytes 196
  7.2 10.9 %copy-start.20 = (s32[1,16]{1,0:T(1,128)S(1)}, s32[1,16]{1,0:T(1,128)}, u32[]{:S(2)}) copy-start(s32[1,16]{1,0:T(1,128)} %param.21) | copy-start | bytes 196
  7.2 10.9 %copy-start.22 = (s32[1,1,128]{2,1,0:T(1,128)S(1)}, s32[1,1,128]{2,1,0:T(1,128)}, u32[]{:S(2)}) copy-start(s32[1,1,128]{2,1,0:T(1,128)} %param.19) | copy-start | bytes 1540
  11.6 16.8 %all-to-all-start = ((bf16[8,16,1152]{2,1,0:T(8,128)(2,1)}), bf16[8,16,1152]{2,1,0:T(8,128)(2,1)S(1)}, u32[]{:S(2)}, u32[]{:S(2)}) async-start(bf16[8,16,1152]{2,1,0:T(8,128)(2,1)} %bitcast.3), calls=%async_computation | async-start | bytes 589824 | tf_op jit(solution)/shard_map/all_to_all | solution.py:51
  18.0 48.1 %all-gather.4.cloned.1.call-start = ((), (), s32[]{:S(2)}) async-start(), calls=%async_computation.2 | async-start | bytes 2654208 | tf_op jit(solution)/shard_map/all_gather | solution.py:77
  18.7 4.5 %copy-start.19 = (s32[1,128]{1,0:T(1,128)S(1)}, s32[1,128]{1,0:T(1,128)}, u32[]{:S(2)}) copy-start(s32[1,128]{1,0:T(1,128)} %param.20) | copy-start | bytes 1540
  24.1 10.2 %copy-start.3 = (f32[128,3456]{1,0:T(8,128)}, f32[128,3456]{1,0:T(8,128)S(1)}, u32[]{:S(2)}) copy-start(f32[128,3456]{1,0:T(8,128)S(1)} %fusion.71) | copy-start | bytes 5308420
  30.1 3.5 copy-start.8
  30.1 4.3 %copy-start.5 = (bf16[1,128,1152]{2,1,0:T(8,128)(2,1)S(1)}, bf16[1,128,1152]{2,1,0:T(8,128)(2,1)}, u32[]{:S(2)}) copy-start(bf16[1,128,1152]{2,1,0:T(8,128)(2,1)} %param.27) | copy-start | bytes 884740
  34.3 82.0 %all-gather.6.cloned.1.call-start = ((), (), s32[]{:S(2)}) async-start(), calls=%async_computation.3 | async-start | bytes 2654208 | tf_op jit(solution)/shard_map/all_gather | solution.py:156
  49.4 301.5 %all-reduce.3.cloned.1.call-start = ((), (), s32[]{:S(2)}) async-start(), calls=%async_computation.4 | async-start | bytes 21233664 | tf_op jit(solution)/shard_map/psum | solution.py:191
  66.1 34.8 %copy-start.15 = (f32[128,8,72]{0,2,1:T(8,128)S(1)}, f32[128,8,72]{0,2,1:T(8,128)}, u32[]{:S(2)}) copy-start(f32[128,8,72]{0,2,1:T(8,128)} %custom-call.2) | copy-start | bytes 884740
  86.4 26.7 %copy-start.10 = (bf16[128,8,72]{0,2,1:T(8,128)(2,1)}, bf16[128,8,72]{0,2,1:T(8,128)(2,1)S(1)}, u32[]{:S(2)}) copy-start(bf16[128,8,72]{0,2,1:T(8,128)(2,1)S(1)} %get-tuple-element.387) | copy-start | bytes 442372
  101.1 3.1 copy-start.16
  107.2 3.1 copy-start.16
  113.1 12.9 %copy-start.12 = (bf16[128,8,72]{0,2,1:T(8,128)(2,1)}, bf16[128,8,72]{0,2,1:T(8,128)(2,1)S(1)}, u32[]{:S(2)}) copy-start(bf16[128,8,72]{0,2,1:T(8,128)(2,1)S(1)} %multiply_convert_fusion.2) | copy-start | bytes 442372
  116.3 1.9 copy-start.17
  116.3 1.9 copy-start.18
  119.5 1.9 copy-start.2
  121.5 4.5 %copy-start.9 = (bf16[128,1152]{1,0:T(8,128)(2,1)S(1)}, bf16[128,1152]{1,0:T(8,128)(2,1)}, u32[]{:S(2)}) copy-start(bf16[128,1152]{1,0:T(8,128)(2,1)} %copy-done.8) | copy-start | bytes 884740
  131.2 1.5 copy-start.4
  131.2 1.5 copy-start.13
  131.2 1.5 copy-start.14
  132.7 3.2 copy-start.6
  132.7 9.6 %copy-start.23 = (s32[1,1,128]{2,1,0:T(1,128)S(1)}, s32[1,1,128]{2,1,0:T(1,128)}, u32[]{:S(2)}) copy-start(s32[1,1,128]{2,1,0:T(1,128)} %param.18) | copy-start | bytes 1540
  135.8 6.5 %copy-start.11 = (bf16[128,8,72]{0,2,1:T(8,128)(2,1)S(1)}, bf16[128,8,72]{0,2,1:T(8,128)(2,1)}, u32[]{:S(2)}) copy-start(bf16[128,8,72]{0,2,1:T(8,128)(2,1)} %copy-done.10) | copy-start | bytes 442372
  137.9 17.5 %all-to-all-start.1 = ((bf16[8,16,1152]{2,1,0:T(8,128)(2,1)}), bf16[8,16,1152]{2,1,0:T(8,128)(2,1)S(1)}, u32[]{:S(2)}, u32[]{:S(2)}) async-start(bf16[8,16,1152]{2,1,0:T(8,128)(2,1)} %bitcast.31), calls=%async_computation.1 | async-start | bytes 589824 | tf_op jit(solution)/shard_map/all_to_all | solution.py:204
  350.9 6.0 %copy-start.7 = (f32[576,1152]{1,0:T(8,128)S(1)}, f32[576,1152]{1,0:T(8,128)}, u32[]{:S(2)}) copy-start(f32[576,1152]{1,0:T(8,128)} %get-tuple-element.385) | copy-start | bytes 7962628
  350.9 7.2 %copy-start.1 = (bf16[1001,1152]{1,0:T(8,128)(2,1)S(1)}, bf16[1001,1152]{1,0:T(8,128)(2,1)}, u32[]{:S(2)}) copy-start(bf16[1001,1152]{1,0:T(8,128)(2,1)} %param.23) | copy-start | bytes 6918916
Sparse Core Ops, SparseCore 0:
  34.4 31.6 all-gather.3
  68.3 31.8 all-gather.5
  131.3 219.5 all-reduce.2
where the time goes:
time: 365 us
  waiting for transfers between devices  225 us (62%)
  matrix products  43.1 us (12%)
  blocking collectives  38.5 us (11%)
  local copies, waits for them, and re-layouts  18.2 us (5%)
  other arithmetic  14.5 us (4%)
  between operations  14.1 us (4%)
  starting transfers between devices  10.9 us (3%)
    psum x1, waiting for transfers between devices, shards(): lax.psum((in_weight_term, out_weight_term), ('grp', 'seq'))  194 us
    all_gather x1, waiting for transfers between devices, shards(): lax.all_gather(key_value, 'seq', axis=0, tiled=True)  16.6 us
    all_gather x1, blocking collectives, shards(): lax.all_gather(delta_rows, 'seq', axis=0, tiled=True)  14.5 us
    all_gather x1, blocking collectives, shards(): lax.all_gather(totals, 'seq', axis=0, tiled=True)  14.3 us
    all_to_all x1, waiting for transfers between devices, shards(): lax.all_to_all(back_order, 'seq', split_axis=0, concat_axis=0, tiled=True)  10.5 us
    all_gather x1, blocking collectives, shards(): lax.all_gather(local_images, 'seq', axis=0, tiled=True)  9.77 us
  transfers between devices with their start and end apart: 5, of which 4 were waited for; matrix products, arithmetic and copies ran while one was open for 12% of the time, Pallas kernels for 0%

commit v1 on v0

v1 whole, which is shorter than its diff:
```python
import functools
import math

import jax
import jax.numpy as jnp
from jax import lax
from jax.experimental import pallas as pl
from jax.experimental.pallas import tpu as pltpu
from jax.sharding import PartitionSpec as P

HEADS = 8
CLASSES = 1000


EPSILON = 1e-06
CONTRACT_LAST = (((1,), (1,)), ((), ()))


def normalize(values):
    center = values - jnp.mean(values, axis=-1, keepdims=True)
    spread = jnp.mean(center * center, axis=-1, keepdims=True)
    inverse_spread = lax.rsqrt(spread + EPSILON)
    return (center * inverse_spread, inverse_spread)


def exponent(query_heads, key_heads, image_query, image_keys, factor):
    logits = (
        jnp.einsum("qhe,khe->qhk", query_heads, key_heads, preferred_element_type=jnp.float32)
        * factor
    )
    joined = (image_query[:, None] == image_keys[None, :])[:, None, :]
    return jnp.exp(jnp.where(joined, logits, -jnp.inf))


def head_kernel(factor, block_rows, image_row, packed_ref, out_ref, flat_ref):
    shard_count, _, padded, tokens = packed_ref.shape
    total_rows = shard_count * tokens
    queries, keys, values, cotangents = (
        jnp.concatenate([packed_ref[s, part] for s in range(shard_count)], axis=1)
        for part in range(4)
    )
    key_columns = keys.T
    value_columns = values.T
    images = cotangents.astype(jnp.float32)[image_row : image_row + 8]
    image_column = images.T[:, :1]
    image_line = images[:1]
    key_sum = jnp.zeros((padded, total_rows), jnp.float32)
    value_sum = jnp.zeros((padded, total_rows), jnp.float32)
    attended_parts, query_parts = [], []
    for start in range(0, total_rows, block_rows):
        stop = start + block_rows
        query_block = queries[:, start:stop]
        cotangent_block = cotangents[:, start:stop]
        logits = jnp.dot(key_columns, query_block, preferred_element_type=jnp.float32)
        joined = image_column == image_line[:, start:stop]
        powers = jnp.where(joined, jnp.exp2(logits * (factor * math.log2(math.e))), 0.0)
        weights = powers * (1.0 / jnp.sum(powers, axis=0, keepdims=True))
        weights_low = weights.astype(jnp.bfloat16)
        attended = jnp.dot(values, weights_low, preferred_element_type=jnp.float32)
        attended_parts.append(attended.astype(jnp.bfloat16))
        attended_low = attended_parts[-1].astype(jnp.float32)
        delta = jnp.sum(
            cotangent_block.astype(jnp.float32) * attended_low, axis=0, keepdims=True
        )
        weight_cotangent = jnp.dot(
            value_columns, cotangent_block, preferred_element_type=jnp.float32
        )
        score_cotangent = (weights * (weight_cotangent - delta)).astype(jnp.bfloat16)
        query_parts.append(
            jnp.dot(keys, score_cotangent, preferred_element_type=jnp.float32) * factor
        )
        key_sum = key_sum + lax.dot_general(
            query_block, score_cotangent, CONTRACT_LAST, preferred_element_type=jnp.float32
        )
        value_sum = value_sum + lax.dot_general(
            cotangent_block, weights_low, CONTRACT_LAST, preferred_element_type=jnp.float32
        )
    results = (
        jnp.concatenate(attended_parts, axis=1),
        jnp.concatenate(query_parts, axis=1).astype(jnp.bfloat16),
        (key_sum * factor).astype(jnp.bfloat16),
        value_sum.astype(jnp.bfloat16),
    )
    for part, result in enumerate(results):
        flat_ref[part] = result
        for s in range(shard_count):
            out_ref[s, part] = result[:, s * tokens : (s + 1) * tokens]


def by_heads(hidden, attention_in, attention_out, branch, local_images, factor, scale):
    tokens = hidden.shape[0]
    head_width = attention_out.shape[0] // HEADS
    padded = -(-(head_width + 8) // 16) * 16
    projected = lax.dot_general(
        attention_in, hidden, (((0,), (1,)), ((), ())), preferred_element_type=jnp.float32
    ).astype(jnp.bfloat16)
    attended_cotangent = lax.dot_general(
        attention_out, branch, CONTRACT_LAST, preferred_element_type=jnp.float32
    ).astype(jnp.bfloat16)
    parts = jnp.concatenate([projected, attended_cotangent], axis=0)
    parts = parts.reshape(4, HEADS, head_width, tokens).transpose(1, 0, 2, 3)
    tail = jnp.zeros((1, 4, 1, 1), jnp.bfloat16).at[0, 3].set(1)
    tail = jnp.broadcast_to(
        tail * local_images.astype(jnp.bfloat16), (HEADS, 4, padded - head_width, tokens)
    )
    sent = jnp.concatenate([parts, tail], axis=2)
    heads = lax.all_to_all(sent, "seq", split_axis=0, concat_axis=0, tiled=True)
    total_rows = heads.shape[0] * tokens
    all_rows = lax.all_gather(
        jnp.concatenate([hidden, branch], axis=1), "seq", axis=0, tiled=True
    )
    results, flat = pl.pallas_call(
        functools.partial(head_kernel, factor, math.gcd(total_rows, 256), head_width),
        out_shape=(
            jax.ShapeDtypeStruct(heads.shape, jnp.bfloat16),
            jax.ShapeDtypeStruct((4, padded, total_rows), jnp.bfloat16),
        ),
        in_specs=[pl.BlockSpec(memory_space=pltpu.VMEM)],
        out_specs=(pl.BlockSpec(memory_space=pltpu.VMEM),) * 2,
    )(heads)
    model_width = hidden.shape[1]
    out_term = jnp.dot(
        flat[0, :head_width], all_rows[:, model_width:], preferred_element_type=jnp.float32
    )
    in_term = jnp.dot(
        flat[1:, :head_width].reshape(3 * head_width, total_rows),
        all_rows[:, :model_width],
        preferred_element_type=jnp.float32,
    )
    terms = jnp.concatenate([out_term, in_term], axis=0).astype(jnp.bfloat16)
    terms = lax.all_to_all(
        terms.reshape(4, head_width, model_width), "grp", split_axis=0, concat_axis=0, tiled=True
    )
    share = (jnp.sum(terms.astype(jnp.float32), axis=0) * scale).astype(jnp.bfloat16)
    joined = lax.all_gather(share, ("grp", "seq"), axis=0, tiled=True)
    inner_width = HEADS * head_width
    gradient_in = joined[inner_width:].T
    gradient_out = joined[:inner_width]
    returned = lax.all_to_all(results, "seq", split_axis=0, concat_axis=0, tiled=True)
    returned = returned[:, :, :head_width].transpose(1, 0, 2, 3)
    attended = returned[0].reshape(HEADS * head_width, tokens)
    input_cotangent = returned[1:].reshape(3 * HEADS * head_width, tokens)
    return attended, input_cotangent, gradient_in, gradient_out


def by_tokens(hidden, attention_in, attention_out, branch, local_images, factor, scale):
    tokens = hidden.shape[0]
    inner_width = attention_out.shape[0]
    head_width = inner_width // HEADS
    projected_in = jnp.dot(hidden, attention_in, preferred_element_type=jnp.float32).astype(
        jnp.bfloat16
    )
    queries = projected_in[:, :inner_width]
    key_value = projected_in[:, inner_width:]
    all_key_value, all_images = (
        lax.all_gather(key_value, "seq", axis=0, tiled=True),
        lax.all_gather(local_images, "seq", axis=0, tiled=True),
    )
    total_rows = all_key_value.shape[0]
    block_rows = math.gcd(total_rows, 512)
    block_count = total_rows // block_rows
    query_heads = queries.reshape(tokens, HEADS, head_width)

    def key_block(block_index):
        first_row = block_index * block_rows
        block_pair = lax.dynamic_slice_in_dim(all_key_value, first_row, block_rows, 0)
        block_images = lax.dynamic_slice_in_dim(all_images, first_row, block_rows, 0)
        key_heads = block_pair[:, :inner_width].reshape(block_rows, HEADS, head_width)
        value_heads = block_pair[:, inner_width:].reshape(block_rows, HEADS, head_width)
        return (key_heads, value_heads, block_images)

    def forward_step(block_index, carried):
        weighted, totals = carried
        key_heads, value_heads, block_images = key_block(block_index)
        powers = exponent(query_heads, key_heads, local_images, block_images, factor)
        totals = totals + jnp.sum(powers, axis=-1)
        weighted = weighted + jnp.einsum(
            "qhk,khe->qhe",
            powers.astype(jnp.bfloat16),
            value_heads,
            preferred_element_type=jnp.float32,
        )
        return (weighted, totals)

    start_state = (
        jnp.zeros((tokens, HEADS, head_width), jnp.float32),
        jnp.zeros((tokens, HEADS), jnp.float32),
    )
    weighted, totals = lax.fori_loop(0, block_count, forward_step, start_state)
    attended = (weighted / totals[:, :, None]).reshape(tokens, inner_width).astype(jnp.bfloat16)
    contract_last = (((1,), (1,)), ((), ()))
    attended_cotangent = lax.dot_general(
        branch, attention_out, contract_last, preferred_element_type=jnp.float32
    ).astype(jnp.bfloat16)
    cotangent_heads = attended_cotangent.reshape(tokens, HEADS, head_width)
    attended_heads = attended.reshape(tokens, HEADS, head_width)
    delta_rows = jnp.sum(
        cotangent_heads.astype(jnp.float32) * attended_heads.astype(jnp.float32), axis=-1
    )

    def query_step(block_index, carried):
        key_heads, value_heads, block_images = key_block(block_index)
        weights = (
            exponent(query_heads, key_heads, local_images, block_images, factor)
            / totals[:, :, None]
        )
        weight_cotangent = jnp.einsum(
            "qhe,khe->qhk", cotangent_heads, value_heads, preferred_element_type=jnp.float32
        )
        score_cotangent = (weights * (weight_cotangent - delta_rows[:, :, None])).astype(
            jnp.bfloat16
        )
        return carried + jnp.einsum(
            "qhk,khe->qhe", score_cotangent, key_heads, preferred_element_type=jnp.float32
        )

    query_sum = lax.fori_loop(
        0, block_count, query_step, jnp.zeros((tokens, HEADS, head_width), jnp.float32)
    )
    all_totals, all_delta = (
        lax.all_gather(totals, "seq", axis=0, tiled=True),
        lax.all_gather(delta_rows, "seq", axis=0, tiled=True),
    )
    local_keys = key_value[:, :inner_width].reshape(tokens, HEADS, head_width)
    local_values = key_value[:, inner_width:].reshape(tokens, HEADS, head_width)
    query_pair = jnp.concatenate([queries, attended_cotangent], axis=1)
    piece_rows = lax.all_gather(query_pair, "seq", axis=0, tiled=True)
    piece_images = lax.all_gather(local_images, "seq", axis=0, tiled=True)
    row_count = piece_rows.shape[0]
    piece_queries = piece_rows[:, :inner_width].reshape(row_count, HEADS, head_width)
    piece_cotangent = piece_rows[:, inner_width:].reshape(row_count, HEADS, head_width)
    weights = (
        exponent(piece_queries, local_keys, piece_images, local_images, factor)
        / all_totals[:, :, None]
    )
    weight_cotangent = jnp.einsum(
        "qhe,khe->qhk", piece_cotangent, local_values, preferred_element_type=jnp.float32
    )
    score_cotangent = (weights * (weight_cotangent - all_delta[:, :, None])).astype(jnp.bfloat16)
    key_part = jnp.einsum(
        "qhk,qhe->khe", score_cotangent, piece_queries, preferred_element_type=jnp.float32
    )
    value_part = jnp.einsum(
        "qhk,qhe->khe",
        weights.astype(jnp.bfloat16),
        piece_cotangent,
        preferred_element_type=jnp.float32,
    )
    key_sum = key_part.reshape(tokens, inner_width)
    value_sum = value_part.reshape(tokens, inner_width)
    input_cotangent = jnp.concatenate(
        [
            (query_sum * factor).reshape(tokens, inner_width).astype(jnp.bfloat16),
            (key_sum * factor).astype(jnp.bfloat16),
            value_sum.astype(jnp.bfloat16),
        ],
        axis=1,
    )
    out_weight_term = jnp.dot(attended.T, branch, preferred_element_type=jnp.float32)
    in_weight_term = jnp.dot(hidden.T, input_cotangent, preferred_element_type=jnp.float32)
    in_summed, out_summed = lax.psum((in_weight_term, out_weight_term), ("grp", "seq"))
    return (
        attended.T,
        input_cotangent.T,
        (in_summed * scale).astype(jnp.bfloat16),
        (out_summed * scale).astype(jnp.bfloat16),
    )


def shards(
    owned_patches,
    send_rows,
    receive_slot,
    segment_ids,
    class_label,
    drop_mask,
    class_table,
    modulation_weight,
    attention_in,
    attention_out,
    cotangent,
):
    shard_count = lax.axis_size("seq")
    tokens = owned_patches.shape[1]
    model_width = owned_patches.shape[2]
    inner_width = attention_out.shape[0]
    head_width = inner_width // HEADS
    factor = head_width ** (-0.5)
    outgoing = jnp.take(owned_patches[0], send_rows[0, 0], axis=0)
    incoming = lax.all_to_all(outgoing, "seq", split_axis=0, concat_axis=0, tiled=True)
    packed = jnp.take(incoming, receive_slot[0, 0], axis=0)
    chosen = jnp.where(drop_mask[0] == 1, CLASSES, class_label[0])
    condition = jnp.take(class_table, chosen, axis=0)
    activated = jax.nn.silu(condition.astype(jnp.float32)).astype(jnp.bfloat16)
    modulation = jnp.dot(activated, modulation_weight, preferred_element_type=jnp.float32)
    local_images = segment_ids[0]
    image_count = class_label.shape[1]
    one_hot = (local_images[:, None] == jnp.arange(image_count, dtype=jnp.int32)[None, :]).astype(
        jnp.float32
    )
    per_token = jnp.dot(
        one_hot, modulation, precision=lax.Precision.HIGHEST, preferred_element_type=jnp.float32
    )
    shift_rows = per_token[:, :model_width]
    scale_rows = per_token[:, model_width : 2 * model_width]
    gate_rows = per_token[:, 2 * model_width :]
    row_values = packed.astype(jnp.float32)
    normed, inverse_spread = normalize(row_values)
    hidden = (normed * (1.0 + scale_rows) + shift_rows).astype(jnp.bfloat16)
    upstream = cotangent[0].astype(jnp.float32)
    branch = (gate_rows * upstream).astype(jnp.bfloat16)
    norm_factor = (lax.axis_size("grp") * shard_count * tokens) ** (-0.5)
    split = by_heads if shard_count == HEADS and lax.axis_size("grp") == 4 else by_tokens
    attended, input_cotangent, gradient_in, gradient_out = split(
        hidden, attention_in, attention_out, branch, local_images, factor, norm_factor
    )
    projected = lax.dot_general(
        attended, attention_out, (((0,), (0,)), ((), ())), preferred_element_type=jnp.float32
    )
    layer_output = (row_values + gate_rows * projected).astype(jnp.bfloat16)
    hidden_cotangent = lax.dot_general(
        input_cotangent,
        attention_in,
        (((0,), (1,)), ((), ())),
        preferred_element_type=jnp.float32,
    )
    scaled_cot = hidden_cotangent * (1.0 + scale_rows)
    packed_cotangent = upstream + inverse_spread * (
        scaled_cot
        - jnp.mean(scaled_cot, axis=-1, keepdims=True)
        - normed * jnp.mean(scaled_cot * normed, axis=-1, keepdims=True)
    )
    packed_low = packed_cotangent.astype(jnp.bfloat16)
    back_order = jnp.zeros_like(packed_low).at[receive_slot[0, 0]].set(packed_low)
    returned = lax.all_to_all(back_order, "seq", split_axis=0, concat_axis=0, tiled=True)
    owner_gradient = jnp.zeros_like(returned).at[send_rows[0, 0]].set(returned)
    return (
        layer_output[None],
        owner_gradient[None],
        gradient_in,
        gradient_out,
    )


def solution(mesh):
    return jax.shard_map(
        shards,
        mesh=mesh,
        in_specs=(
            P("grp", "seq", None),
            P("grp", "seq", None),
            P("grp", "seq", None),
            P("grp", "seq"),
            P("grp", None),
            P("grp", None),
            P(),
            P(),
            P(),
            P(),
            P("grp", "seq", None),
        ),
        out_specs=(P("grp", "seq", None), P("grp", "seq", None), P(), P()),
        check_vma=False,
    )
```

time: 365 us -> 197 us (0.54)
  waiting for transfers between devices: 225 us -> 59.8 us
  matrix products: 43.1 us -> 22.6 us
  blocking collectives: 38.5 us -> 52.8 us
  Pallas kernels: 0 us -> 7.24 us
  other arithmetic: 14.5 us -> 9.69 us
    psum x1 -> x0, waiting for transfers between devices: 194 us -> none  [shards(): lax.psum((in_weight_term, out_weight_term), ('grp', 'seq'))]
    all_to_all x0 -> x2, blocking collectives: none -> 52.8 us  [the longest x1 38.6 us: by_heads(): heads = lax.all_to_all(sent, 'seq', split_axis=0, concat_axis=0, tiled=True)]
    all_gather x3 -> x0, blocking collectives: 38.5 us -> none  [the longest x1 14.5 us: shards(): lax.all_gather(delta_rows, 'seq', axis=0, tiled=True)]
    dot_general x17 -> x6, matrix products: 37.8 us -> 16 us  [the longest x1 3.61 us: by_heads(): lax.dot_general(attention_in, hidden, (((0,), (1,)), ((), ())), preferred...]
    all_to_all x0 -> x1, waiting for transfers between devices: none -> 21.4 us  [by_heads(): lax.all_to_all(results, 'seq', split_axis=0, concat_axis=0, tiled=True)]
    all_gather x2, waiting for transfers between devices: 16.6 us -> 27.5 us  [the longest x1 18.6 us: by_heads(): joined = lax.all_gather(share, ('grp', 'seq'), axis=0, tiled=True)]
    pallas_call x0 -> x1, Pallas kernels: none -> 7.24 us  [by_heads(): pl.pallas_call(functools.partial(head_kernel, factor, math.gcd(total_rows...]
    convert_element_type x3 -> x2, other arithmetic: 7.26 us -> 0.69 us  [the longest x1 0.68 us: by_heads(): (jnp.sum(terms.astype(jnp.float32), axis=0) * scale).astype(jnp.bfloat16)]
  transfers between devices with their start and end apart: 5 -> 5, of which waited for: 4 -> 5; matrix products, arithmetic and copies ran while one was open for 12% -> 13% of each run, Pallas kernels for 0% -> 4%
where the time goes in v1:
time: 197 us
  waiting for transfers between devices  59.8 us (30%)
  blocking collectives  52.8 us (27%)
  matrix products  22.6 us (11%)
  local copies, waits for them, and re-layouts  15.8 us (8%)
  between operations  15.1 us (8%)
  starting transfers between devices  13.6 us (7%)
  other arithmetic  9.69 us (5%)
  Pallas kernels  7.24 us (4%)
    all_to_all x1, blocking collectives, by_heads(): heads = lax.all_to_all(sent, 'seq', split_axis=0, concat_axis=0, tiled=True)  38.6 us
    all_to_all x1, waiting for transfers between devices, by_heads(): lax.all_to_all(results, 'seq', split_axis=0, concat_axis=0, tiled=True)  21.4 us
    all_gather x1, waiting for transfers between devices, by_heads(): joined = lax.all_gather(share, ('grp', 'seq'), axis=0, tiled=True)  18.6 us
    all_to_all x1, blocking collectives, by_heads(): lax.all_to_all(terms.reshape(4, head_width, model_width), 'grp', split_ax...  14.2 us
    all_gather x1, waiting for transfers between devices, by_heads(): lax.all_gather(jnp.concatenate([hidden, branch], axis=1), 'seq', axis=0,...  8.93 us
    all_to_all x1, waiting for transfers between devices, shards(): lax.all_to_all(back_order, 'seq', split_axis=0, concat_axis=0, tiled=True)  7.8 us
    pallas_call x1, Pallas kernels, by_heads(): pl.pallas_call(functools.partial(head_kernel, factor, math.gcd(total_rows...  7.24 us
    all_to_all x1, starting transfers between devices, shards(): lax.all_to_all(outgoing, 'seq', split_axis=0, concat_axis=0, tiled=True)  6.35 us
  transfers between devices with their start and end apart: 5, of which 5 were waited for; matrix products, arithmetic and copies ran while one was open for 13% of the time, Pallas kernels for 4%

profile of v1, /device:TPU:0, one launch (start us, length us, event | category | flops | bytes accessed | tf_op | source)
XLA Modules:
  0.0 196.5 jit_solution(5101645420222931876)
XLA Ops:
  7.2 0.8 compare_and_fusion.1
  8.7 2.1 %gather_fusion.1 = bf16[128,1152]{1,0:T(8,128)(2,1)S(1)} fusion(bf16[128,1152]{1,0:T(8,128)(2,1)} %bitcast.74, s32[1024]{0:T(1024)S(1)} %pad_clamp_fusion.2), kind=kCustom, calls=%fused_computation.clone | custom fusion | bytes 590336 | tf_op jit(solution)/shard_map/jit(_take)/gather | solution.py:289
  10.8 0.8 broadcast_select_fusion.1
  11.6 6.4 %all-to-all-start = ((bf16[8,16,1152]{2,1,0:T(8,128)(2,1)}), bf16[8,16,1152]{2,1,0:T(8,128)(2,1)S(1)}, u32[]{:S(2)}, u32[]{:S(2)}) async-start(bf16[8,16,1152]{2,1,0:T(8,128)(2,1)} %bitcast.3), calls=%async_computation | async-start | bytes 589824 | tf_op jit(solution)/shard_map/all_to_all | solution.py:290
  18.7 4.5 %fusion.41 = f32[16,3456]{1,0:T(8,128)S(1)} fusion(bf16[1152,3456]{1,0:T(8,128)(2,1)} %param.22, bf16[16,1152]{1,0:T(8,128)(2,1)S(1)} %gather_fusion, pred[16]{0:T(512)(128)(4,1)S(1)} %compare_and_fusion.2), kind=kOutput, calls=%fused_computation.67 | convolution fusion | flops 127531008 | bytes 8220688 | tf_op jit(solution)/shard_map/dot_general | solution.py:295
  23.3 2.1 %fusion.40 = f32[128,3456]{1,0:T(8,128)} fusion(f32[16,3456]{1,0:T(8,128)S(1)} %fusion.41, s32[128]{0:T(128)S(1)} %bitcast.84), kind=kOutput, calls=%fused_computation.66 | convolution fusion | flops 84936704 | bytes 1991168 | tf_op jit(solution)/shard_map/dot_general | solution.py:301
  25.4 3.0 %all-to-all-done = bf16[8,16,1152]{2,1,0:T(8,128)(2,1)S(1)} async-done(((bf16[8,16,1152]{2,1,0:T(8,128)(2,1)}), bf16[8,16,1152]{2,1,0:T(8,128)(2,1)S(1)}, u32[]{:S(2)}, u32[]{:S(2)}) %all-to-all-start) | async-done | bytes 294944 | tf_op jit(solution)/shard_map/all_to_all | solution.py:290
  28.4 0.9 gather_fusion.2
  29.8 1.7 fusion.17
  31.6 0.9 pad_maximum_fusion.3
  34.5 0.8 scatter.19
  35.3 1.8 fusion.10
  37.2 3.6 %fusion.5 = bf16[1728,128]{1,0:T(8,128)(2,1)S(1)} fusion(bf16[128,1152]{1,0:T(8,128)(2,1)S(1)} %get-tuple-element.23, bf16[1152,1728]{0,1:T(8,128)(2,1)} %param.23), kind=kOutput, calls=%fused_computation.15 | convolution fusion | flops 509829120 | bytes 4718592 | tf_op jit(solution)/shard_map/dot_general | solution.py:94
  41.0 38.6 %all_to_all.39.packed_ref = bf16[8,4,80,128]{3,2,1,0:T(8,128)(2,1)} all-to-all(bf16[8,4,80,128]{3,2,1,0:T(8,128)(2,1)S(1)} %pad_maximum_fusion.1), channel_id=1, replica_groups=mesh['grp'=4,'seq'=8] {'seq'}, dimensions={0} | all-to-all | bytes 1310720 | tf_op jit(solution)/shard_map/all_to_all | solution.py:107
  79.5 7.2 %shard_map.138 = (bf16[8,4,80,128]{3,2,1,0:T(8,128)(2,1)}, bf16[4,80,1024]{2,1,0:T(8,128)(2,1)}) custom-call(bf16[8,4,80,128]{3,2,1,0:T(8,128)(2,1)} %all_to_all.39.packed_ref), custom_call_target="tpu_custom_call" | custom-call | tf_op jit(solution)/shard_map/pallas_call | solution.py:112
  86.8 1.1 slice.75
  87.9 8.9 %all-gather.3.cloned.1.call-done = bf16[1024,2304]{1,0:T(8,128)(2,1)} async-done(((bf16[128,2304]{1,0:T(8,128)(2,1)}), bf16[1024,2304]{1,0:T(8,128)(2,1)}) %all-gather.3.cloned.1.call-update) | async-done | bytes 4718608 | tf_op jit(solution)/shard_map/all_gather | solution.py:109
  96.8 2.3 %fusion.7 = bf16[72,1152]{1,0:T(8,128)(2,1)S(1)} fusion(bf16[1024,2304]{1,0:T(8,128)(2,1)} %all-gather.3.cloned.1.call-done, bf16[4,80,1024]{2,1,0:T(8,128)(2,1)} %get-tuple-element.20), kind=kOutput, calls=%fused_computation.17 | convolution fusion | flops 169952256 | bytes 2672640 | tf_op jit(solution)/shard_map/dot_general | solution.py:122
  99.1 2.4 %convolution_convert_fusion = bf16[216,1152]{1,0:T(8,128)(2,1)S(1)} fusion(bf16[216,1024]{1,0:T(8,128)(2,1)S(1)} %bitcast.81, bf16[1024,2304]{1,0:T(8,128)(2,1)} %all-gather.3.cloned.1.call-done), kind=kOutput, calls=%fused_computation.6 | convolution fusion | flops 509856768 | bytes 3299328 | tf_op jit(solution)/shard_map/dot_general | solution.py:125
  101.6 14.2 %all_to_all.40 = bf16[4,72,1152]{2,1,0:T(8,128)(2,1)S(1)} all-to-all(bf16[4,72,1152]{2,1,0:T(8,128)(2,1)S(1)} %bitcast.75), channel_id=1, replica_groups=mesh['grp'=4,'seq'=8] {'grp'}, dimensions={0} | all-to-all | bytes 1327104 | tf_op jit(solution)/shard_map/all_to_all | solution.py:131
  116.6 3.7 %all-to-all-start.2 = ((bf16[8,4,80,128]{3,2,1,0:T(8,128)(2,1)}), bf16[8,4,80,128]{3,2,1,0:T(8,128)(2,1)S(1)}, u32[]{:S(2)}, u32[]{:S(2)}) async-start(bf16[8,4,80,128]{3,2,1,0:T(8,128)(2,1)} %get-tuple-element.19), calls=%async_computation.2 | async-start | bytes 1310720 | tf_op jit(solution)/shard_map/all_to_all | solution.py:139
  120.3 21.4 %all-to-all-done.2 = bf16[8,4,80,128]{3,2,1,0:T(8,128)(2,1)S(1)} async-done(((bf16[8,4,80,128]{3,2,1,0:T(8,128)(2,1)}), bf16[8,4,80,128]{3,2,1,0:T(8,128)(2,1)S(1)}, u32[]{:S(2)}, u32[]{:S(2)}) %all-to-all-start.2) | async-done | bytes 655392 | tf_op jit(solution)/shard_map/all_to_all | solution.py:139
  141.8 0.8 copy-done.1
  142.7 3.2 %fusion.53 = (f32[128]{0:T(128)S(1)}, f32[128]{0:T(128)S(1)}, f32[128,1152]{1,0:T(8,128)S(1)}) fusion(f32[128]{0:T(128)S(1)} %add_rsqrt_fusion, f32[128]{0:T(128)S(1)} %broadcast_multiply_fusion.3, bf16[128,1152]{1,0:T(8,128)(2,1)S(1)} %gather_fusion.2, pred[128]{0:T(512)(128)(4,1)S(1)} %compare_and_fusion, f32[128,3456]{1,0:T(8,128)} %fusion.40, ...), kind=kOutput, calls=%fused_computation.99 | convolution fusion | flops 510934784 | bytes 5900416 | tf_op jit(solution)/shard_map/dot_general | solution.py:321
  146.0 2.5 %scatter_custom_fusion = bf16[128,1152]{1,0:T(8,128)(2,1)} fusion(s32[128]{0:T(128)S(1)} %fusion.50, f32[128,1152]{1,0:T(8,128)S(1)} %get-tuple-element.25, bf16[1,128,1152]{2,1,0:T(8,128)(2,1)} %param.25, f32[128]{0:T(128)S(1)} %get-tuple-element.26, f32[128]{0:T(128)S(1)} %get-tuple-element.27, f32[128]{0:T(128)S(1)} %add_rsqrt_fusion, ...), kind=kCustom, calls=%fused_computation.46 | custom fusion | flops 1622016 | bytes 1477122 | tf_op jit(solution)/shard_map/scatter | solution.py:334
  148.5 3.4 %all-to-all-start.3 = ((bf16[8,16,1152]{2,1,0:T(8,128)(2,1)}), bf16[8,16,1152]{2,1,0:T(8,128)(2,1)S(1)}, u32[]{:S(2)}, u32[]{:S(2)}) async-start(bf16[8,16,1152]{2,1,0:T(8,128)(2,1)} %bitcast.80), calls=%async_computation.3 | async-start | bytes 589824 | tf_op jit(solution)/shard_map/all_to_all | solution.py:335
  152.0 2.6 %fusion.6 = bf16[1,128,1152]{2,1,0:T(8,128)(2,1)} fusion(bf16[576,128]{1,0:T(8,128)(2,1)S(1)} %bitcast.76, bf16[576,1152]{1,0:T(8,128)(2,1)} %param.24, f32[128,3456]{1,0:T(8,128)} %fusion.40, bf16[128,1152]{1,0:T(8,128)(2,1)S(1)} %gather_fusion.2, pred[128]{0:T(512)(128)(4,1)S(1)} %compare_and_fusion), kind=kOutput, calls=%fused_computation.16 | convolution fusion | flops 170606592 | bytes 2654336 | tf_op jit(solution)/shard_map/dot_general | solution.py:317
  154.6 7.8 %all-to-all-done.3 = bf16[8,16,1152]{2,1,0:T(8,128)(2,1)S(1)} async-done(((bf16[8,16,1152]{2,1,0:T(8,128)(2,1)}), bf16[8,16,1152]{2,1,0:T(8,128)(2,1)S(1)}, u32[]{:S(2)}, u32[]{:S(2)}) %all-to-all-start.3) | async-done | bytes 294944 | tf_op jit(solution)/shard_map/all_to_all | solution.py:335
  162.4 1.8 scatter_custom_fusion.1
  164.2 18.6 %all-gather.5.cloned.1.call-done = bf16[2304,1152]{1,0:T(8,128)(2,1)} async-done(((bf16[72,1152]{1,0:T(8,128)(2,1)}), bf16[2304,1152]{1,0:T(8,128)(2,1)}) %all-gather.5.cloned.1.call-update) | async-done | bytes 5308432 | tf_op jit(solution)/shard_map/all_gather | solution.py:135
  182.8 2.5 %slice.94 = bf16[576,1152]{1,0:T(8,128)(2,1)} slice(bf16[2304,1152]{1,0:T(8,128)(2,1)} %all-gather.5.cloned.1.call-done), slice={[0:576], [0:1152]} | slice | bytes 2654208 | tf_op jit(solution)/shard_map/slice | solution.py:138
  185.3 4.4 %slice_bitcast_fusion = bf16[1152,1728]{0,1:T(8,128)(2,1)} fusion(bf16[2304,1152]{1,0:T(8,128)(2,1)} %all-gather.5.cloned.1.call-done), kind=kLoop, calls=%fused_computation.5 | loop fusion | bytes 7962624 | tf_op jit(solution)/shard_map/transpose | solution.py:137
  (55 shorter events, 4.4 us)
Async XLA Ops:
  7.2 11.0 %copy-start = (bf16[1001,1152]{1,0:T(8,128)(2,1)S(1)}, bf16[1001,1152]{1,0:T(8,128)(2,1)}, u32[]{:S(2)}) copy-start(bf16[1001,1152]{1,0:T(8,128)(2,1)} %param.21) | copy-start | bytes 6918916
  7.2 10.9 %copy-start.6 = (s32[1,16]{1,0:T(1,128)S(1)}, s32[1,16]{1,0:T(1,128)}, u32[]{:S(2)}) copy-start(s32[1,16]{1,0:T(1,128)} %param.20) | copy-start | bytes 196
  7.2 10.9 %copy-start.5 = (s32[1,16]{1,0:T(1,128)S(1)}, s32[1,16]{1,0:T(1,128)}, u32[]{:S(2)}) copy-start(s32[1,16]{1,0:T(1,128)} %param.19) | copy-start | bytes 196
  7.2 10.9 %copy-start.7 = (s32[1,1,128]{2,1,0:T(1,128)S(1)}, s32[1,1,128]{2,1,0:T(1,128)}, u32[]{:S(2)}) copy-start(s32[1,1,128]{2,1,0:T(1,128)} %param.17) | copy-start | bytes 1540
  11.6 16.8 %all-to-all-start = ((bf16[8,16,1152]{2,1,0:T(8,128)(2,1)}), bf16[8,16,1152]{2,1,0:T(8,128)(2,1)S(1)}, u32[]{:S(2)}, u32[]{:S(2)}) async-start(bf16[8,16,1152]{2,1,0:T(8,128)(2,1)} %bitcast.3), calls=%async_computation | async-start | bytes 589824 | tf_op jit(solution)/shard_map/all_to_all | solution.py:290
  18.0 78.8 %all-gather.3.cloned.1.call-start = ((), (), s32[]{:S(2)}) async-start(), calls=%async_computation.5 | async-start | bytes 5308416 | tf_op jit(solution)/shard_map/all_gather | solution.py:109
  18.7 4.5 %copy-start.3 = (s32[1,128]{1,0:T(1,128)S(1)}, s32[1,128]{1,0:T(1,128)}, u32[]{:S(2)}) copy-start(s32[1,128]{1,0:T(1,128)} %param.18) | copy-start | bytes 1540
  23.2 6.5 %copy-start.2 = (bf16[1,128,1152]{2,1,0:T(8,128)(2,1)S(1)}, bf16[1,128,1152]{2,1,0:T(8,128)(2,1)}, u32[]{:S(2)}) copy-start(bf16[1,128,1152]{2,1,0:T(8,128)(2,1)} %param.25) | copy-start | bytes 884740
  29.8 3.3 %copy-start.4 = (s32[4]{0:T(128)S(1)}, s32[4]{0:T(128)}, u32[]{:S(2)}) copy-start(s32[4]{0:T(128)} %constant.85.clone.1) | copy-start | bytes 52
  32.4 150.4 %all-gather.5.cloned.1.call-start = ((), (), s32[]{:S(2)}) async-start(), calls=%async_computation.6 | async-start | bytes 5474304 | tf_op jit(solution)/shard_map/all_gather | solution.py:135
  116.6 25.2 %all-to-all-start.2 = ((bf16[8,4,80,128]{3,2,1,0:T(8,128)(2,1)}), bf16[8,4,80,128]{3,2,1,0:T(8,128)(2,1)S(1)}, u32[]{:S(2)}, u32[]{:S(2)}) async-start(bf16[8,4,80,128]{3,2,1,0:T(8,128)(2,1)} %get-tuple-element.19), calls=%async_computation.2 | async-start | bytes 1310720 | tf_op jit(solution)/shard_map/all_to_all | solution.py:139
  141.8 0.8 copy-start.1
  142.7 9.2 %copy-start.8 = (s32[1,1,128]{2,1,0:T(1,128)S(1)}, s32[1,1,128]{2,1,0:T(1,128)}, u32[]{:S(2)}) copy-start(s32[1,1,128]{2,1,0:T(1,128)} %param.16) | copy-start | bytes 1540
  145.9 6.0 %slice-start = ((bf16[4,8,72,128]{3,2,0,1:T(8,128)(2,1)}), bf16[1,8,72,128]{3,2,0,1:T(8,128)(2,1)S(1)}, s32[]{:S(2)}) async-start(bf16[4,8,72,128]{3,2,0,1:T(8,128)(2,1)} %copy-done.1), calls=%async_computation.7 | async-start | bytes 294912 | tf_op jit(solution)/shard_map/slice | solution.py:141
  148.5 13.9 %all-to-all-start.3 = ((bf16[8,16,1152]{2,1,0:T(8,128)(2,1)}), bf16[8,16,1152]{2,1,0:T(8,128)(2,1)S(1)}, u32[]{:S(2)}, u32[]{:S(2)}) async-start(bf16[8,16,1152]{2,1,0:T(8,128)(2,1)} %bitcast.80), calls=%async_computation.3 | async-start | bytes 589824 | tf_op jit(solution)/shard_map/all_to_all | solution.py:335
Sparse Core Ops, SparseCore 0:
  32.6 64.1 all-gather.2
  116.7 66.1 all-gather.4

commit v2 on v1

--- a/solution.py
+++ b/solution.py
@@ -87,6 +87,97 @@
             out_ref[s, part] = result[:, s * tokens : (s + 1) * tokens]
 
 
+def gather_kernel(share_ref, out_ref, local_sem, send_sems, recv_sems):
+    group, place = lax.axis_index("grp"), lax.axis_index("seq")
+    shard_count = out_ref.shape[0] // 4
+    depth = shard_count // 2
+    level, core = place // 2, place % 2
+    groups = [group + bit - 2 * bit * ((group // bit) % 2) for bit in (1, 2)]
+    groups.append(3 - group)
+
+    def place_at(hop):
+        return lax.rem(level + hop, depth) * 2 + core
+
+    sideways = (groups[0], place)
+    upward = (groups[1], place)
+    partner = (group, level * 2 + 1 - core)
+    along = [(group, place_at(hop)) for hop in range(1, depth)]
+    barrier = pltpu.get_barrier_semaphore()
+    for target in [sideways, upward, partner] + along:
+        pl.semaphore_signal(
+            barrier, inc=1, device_id=target, device_id_type=pl.DeviceIdType.MESH
+        )
+    pl.semaphore_wait(barrier, 3 + len(along))
+    started = []
+
+    def send(source, slot, target):
+        copy = pltpu.make_async_remote_copy(
+            src_ref=source,
+            dst_ref=out_ref.at[slot],
+            send_sem=send_sems.at[len(started)],
+            recv_sem=recv_sems.at[slot],
+            device_id=target,
+            device_id_type=pl.DeviceIdType.MESH,
+        )
+        copy.start()
+        started.append(copy)
+
+    def arrive(slot):
+        pltpu.make_async_remote_copy(
+            src_ref=share_ref,
+            dst_ref=out_ref.at[slot],
+            send_sem=send_sems.at[0],
+            recv_sem=recv_sems.at[slot],
+            device_id=partner,
+            device_id_type=pl.DeviceIdType.MESH,
+        ).wait_recv()
+
+    own = group * shard_count + place
+    for target in along + [sideways, upward, partner]:
+        send(share_ref, own, target)
+    keep = pltpu.make_async_copy(share_ref, out_ref.at[own], local_sem)
+    keep.start()
+    for hop in range(depth):
+        if hop:
+            slot = group * shard_count + place_at(hop)
+            arrive(slot)
+            for target in (sideways, upward, partner):
+                send(out_ref.at[slot], slot, target)
+        for side, onward in ((0, upward), (1, sideways)):
+            slot = groups[side] * shard_count + place_at(hop)
+            arrive(slot)
+            if hop % 2 == side:
+                send(out_ref.at[slot], slot, onward)
+            send(out_ref.at[slot], slot, partner)
+    for hop in range(depth):
+        slot = groups[2] * shard_count + place_at(hop)
+        arrive(slot)
+        send(out_ref.at[slot], slot, partner)
+    for other in range(4):
+        for step in range(depth):
+            arrive(other * shard_count + step * 2 + 1 - core)
+    keep.wait()
+    for copy in started:
+        copy.wait_send()
+
+
+def gather_all(share):
+    count = lax.axis_size("grp") * lax.axis_size("seq")
+    gathered = pl.pallas_call(
+        gather_kernel,
+        out_shape=jax.ShapeDtypeStruct((count, *share.shape), share.dtype),
+        in_specs=[pl.BlockSpec(memory_space=pltpu.VMEM)],
+        out_specs=pl.BlockSpec(memory_space=pltpu.VMEM),
+        scratch_shapes=[
+            pltpu.SemaphoreType.DMA,
+            pltpu.SemaphoreType.DMA((count,)),
+            pltpu.SemaphoreType.DMA((count,)),
+        ],
+        compiler_params=pltpu.CompilerParams(collective_id=0, has_side_effects=True),
+    )(share)
+    return gathered.reshape(count * share.shape[0], share.shape[1])
+
+
 def by_heads(hidden, attention_in, attention_out, branch, local_images, factor, scale):
     tokens = hidden.shape[0]
     head_width = attention_out.shape[0] // HEADS
@@ -132,7 +223,7 @@
         terms.reshape(4, head_width, model_width), "grp", split_axis=0, concat_axis=0, tiled=True
     )
     share = (jnp.sum(terms.astype(jnp.float32), axis=0) * scale).astype(jnp.bfloat16)
-    joined = lax.all_gather(share, ("grp", "seq"), axis=0, tiled=True)
+    joined = gather_all(share)
     inner_width = HEADS * head_width
     gradient_in = joined[inner_width:].T
     gradient_out = joined[:inner_width]

time: 197 us -> 201 us (1.020)
  Pallas kernels: 7.24 us -> 49.8 us
  waiting for transfers between devices: 59.8 us -> 28.8 us
  blocking collectives: 52.8 us -> 38.6 us
  starting transfers between devices: 13.6 us -> 17.2 us
    pallas_call x0 -> x1, Pallas kernels: none -> 42.5 us  [gather_all(): pl.pallas_call(gather_kernel, out_shape=jax.ShapeDtypeStruct((count, *sha...]
    all_gather x1 -> x0, waiting for transfers between devices: 18.6 us -> none  [by_heads(): joined = lax.all_gather(share, ('grp', 'seq'), axis=0, tiled=True)]
    all_to_all x1 -> x0, blocking collectives: 14.2 us -> none  [by_heads(): lax.all_to_all(terms.reshape(4, head_width, model_width), 'grp', split_ax...]
    all_gather x1, waiting for transfers between devices: 8.93 us -> 0.02 us  [by_heads(): lax.all_gather(jnp.concatenate([hidden, branch], axis=1), 'seq', axis=0,...]
    all_to_all x1, waiting for transfers between devices: 21.4 us -> 16.9 us  [by_heads(): lax.all_to_all(results, 'seq', split_axis=0, concat_axis=0, tiled=True)]
    slice x0 -> x1, local copies, waits for them, and re-layouts: none -> 4.37 us  [by_heads(): gradient_in = joined[inner_width:].T]
    transpose x1 -> x0, local copies, waits for them, and re-layouts: 4.37 us -> none  [by_heads(): gradient_in = joined[inner_width:].T]
    all_to_all x0 -> x1, waiting for transfers between devices: none -> 4.28 us  [by_heads(): lax.all_to_all(terms.reshape(4, head_width, model_width), 'grp', split_ax...]
  transfers between devices with their start and end apart: 5 -> 5, of which waited for: 5 -> 4; matrix products, arithmetic and copies ran while one was open for 13% -> 16% of each run, Pallas kernels for 4% -> 4%
where the time goes in v2:
time: 201 us; the launch traced here: 200 us
  Pallas kernels  49.8 us (25%)
  blocking collectives  38.6 us (19%)
  waiting for transfers between devices  28.8 us (14%)
  matrix products  22.8 us (11%)
  local copies, waits for them, and re-layouts  17.7 us (9%)
  starting transfers between devices  17.2 us (9%)
  between operations  15 us (7%)
  other arithmetic  10.1 us (5%)
    pallas_call x1, Pallas kernels, gather_all(): pl.pallas_call(gather_kernel, out_shape=jax.ShapeDtypeStruct((count, *sha...  42.5 us
    all_to_all x1, blocking collectives, by_heads(): heads = lax.all_to_all(sent, 'seq', split_axis=0, concat_axis=0, tiled=True)  38.6 us
    all_to_all x1, waiting for transfers between devices, by_heads(): lax.all_to_all(results, 'seq', split_axis=0, concat_axis=0, tiled=True)  16.9 us
    pallas_call x1, Pallas kernels, by_heads(): pl.pallas_call(functools.partial(head_kernel, factor, math.gcd(total_rows...  7.25 us
    all_to_all x1, starting transfers between devices, shards(): lax.all_to_all(outgoing, 'seq', split_axis=0, concat_axis=0, tiled=True)  6.35 us
    all_to_all x1, waiting for transfers between devices, shards(): lax.all_to_all(back_order, 'seq', split_axis=0, concat_axis=0, tiled=True)  4.53 us
    dot_general x1, matrix products, shards(): jnp.dot(activated, modulation_weight, preferred_element_type=jnp.float32)  4.46 us
    slice x1, local copies, waits for them, and re-layouts, by_heads(): gradient_in = joined[inner_width:].T  4.37 us
  transfers between devices with their start and end apart: 5, of which 4 were waited for; matrix products, arithmetic and copies ran while one was open for 16% of the time, Pallas kernels for 4%

profile of v2, /device:TPU:0, one launch (start us, length us, event | category | flops | bytes accessed | tf_op | source)
XLA Modules:
  0.0 200.0 jit_solution(16294540482764648409)
XLA Ops:
  7.2 0.8 compare_and_fusion.1
  8.7 2.1 %gather_fusion.1 = bf16[128,1152]{1,0:T(8,128)(2,1)S(1)} fusion(bf16[128,1152]{1,0:T(8,128)(2,1)} %bitcast.76, s32[1024]{0:T(1024)S(1)} %pad_clamp_fusion.2), kind=kCustom, calls=%fused_computation.clone | custom fusion | bytes 590336 | tf_op jit(solution)/shard_map/jit(_take)/gather | solution.py:380
  10.8 0.8 broadcast_select_fusion.1
  11.6 6.4 %all-to-all-start = ((bf16[8,16,1152]{2,1,0:T(8,128)(2,1)}), bf16[8,16,1152]{2,1,0:T(8,128)(2,1)S(1)}, u32[]{:S(2)}, u32[]{:S(2)}) async-start(bf16[8,16,1152]{2,1,0:T(8,128)(2,1)} %bitcast.3), calls=%async_computation | async-start | bytes 589824 | tf_op jit(solution)/shard_map/all_to_all | solution.py:381
  18.8 4.5 %fusion.41 = f32[16,3456]{1,0:T(8,128)S(1)} fusion(bf16[1152,3456]{1,0:T(8,128)(2,1)} %param.22, bf16[16,1152]{1,0:T(8,128)(2,1)S(1)} %gather_fusion, pred[16]{0:T(512)(128)(4,1)S(1)} %compare_and_fusion.2), kind=kOutput, calls=%fused_computation.66 | convolution fusion | flops 127531008 | bytes 8220688 | tf_op jit(solution)/shard_map/dot_general | solution.py:386
  23.3 2.1 %fusion.40 = f32[128,3456]{1,0:T(8,128)} fusion(f32[16,3456]{1,0:T(8,128)S(1)} %fusion.41, s32[128]{0:T(128)S(1)} %bitcast.87), kind=kOutput, calls=%fused_computation.65 | convolution fusion | flops 84936704 | bytes 1991168 | tf_op jit(solution)/shard_map/dot_general | solution.py:392
  25.4 3.1 %all-to-all-done = bf16[8,16,1152]{2,1,0:T(8,128)(2,1)S(1)} async-done(((bf16[8,16,1152]{2,1,0:T(8,128)(2,1)}), bf16[8,16,1152]{2,1,0:T(8,128)(2,1)S(1)}, u32[]{:S(2)}, u32[]{:S(2)}) %all-to-all-start) | async-done | bytes 294944 | tf_op jit(solution)/shard_map/all_to_all | solution.py:381
  28.4 0.9 gather_fusion.2
  29.8 1.7 fusion.17
  31.6 0.9 pad_maximum_fusion.3
  35.3 1.8 fusion.10
  37.1 3.6 %fusion.5 = bf16[1728,128]{1,0:T(8,128)(2,1)S(1)} fusion(bf16[128,1152]{1,0:T(8,128)(2,1)S(1)} %get-tuple-element.23, bf16[1152,1728]{0,1:T(8,128)(2,1)} %param.23), kind=kOutput, calls=%fused_computation.14 | convolution fusion | flops 509829120 | bytes 4718592 | tf_op jit(solution)/shard_map/dot_general | solution.py:185
  40.9 38.6 %all_to_all.39.packed_ref = bf16[8,4,80,128]{3,2,1,0:T(8,128)(2,1)} all-to-all(bf16[8,4,80,128]{3,2,1,0:T(8,128)(2,1)S(1)} %pad_maximum_fusion.1), channel_id=1, replica_groups=mesh['grp'=4,'seq'=8] {'seq'}, dimensions={0} | all-to-all | bytes 1310720 | tf_op jit(solution)/shard_map/all_to_all | solution.py:198
  79.6 7.3 %shard_map.138 = (bf16[8,4,80,128]{3,2,1,0:T(8,128)(2,1)}, bf16[4,80,1024]{2,1,0:T(8,128)(2,1)}) custom-call(bf16[8,4,80,128]{3,2,1,0:T(8,128)(2,1)} %all_to_all.39.packed_ref), custom_call_target="tpu_custom_call" | custom-call | tf_op jit(solution)/shard_map/pallas_call | solution.py:203
  86.8 3.7 %all-to-all-start.2 = ((bf16[8,4,80,128]{3,2,1,0:T(8,128)(2,1)}), bf16[8,4,80,128]{3,2,1,0:T(8,128)(2,1)S(1)}, u32[]{:S(2)}, u32[]{:S(2)}) async-start(bf16[8,4,80,128]{3,2,1,0:T(8,128)(2,1)} %get-tuple-element.19), calls=%async_computation.2 | async-start | bytes 1310720 | tf_op jit(solution)/shard_map/all_to_all | solution.py:230
  90.6 1.8 slice.81
  92.4 16.9 %all-to-all-done.2 = bf16[8,4,80,128]{3,2,1,0:T(8,128)(2,1)S(1)} async-done(((bf16[8,4,80,128]{3,2,1,0:T(8,128)(2,1)}), bf16[8,4,80,128]{3,2,1,0:T(8,128)(2,1)S(1)}, u32[]{:S(2)}, u32[]{:S(2)}) %all-to-all-start.2) | async-done | bytes 655392 | tf_op jit(solution)/shard_map/all_to_all | solution.py:230
  109.4 0.8 copy-done.1
  110.3 3.3 %fusion.53 = (f32[128]{0:T(128)S(1)}, f32[128]{0:T(128)S(1)}, f32[128,1152]{1,0:T(8,128)S(1)}) fusion(f32[128]{0:T(128)S(1)} %add_rsqrt_fusion, f32[128]{0:T(128)S(1)} %broadcast_multiply_fusion.3, bf16[128,1152]{1,0:T(8,128)(2,1)S(1)} %gather_fusion.2, pred[128]{0:T(512)(128)(4,1)S(1)} %compare_and_fusion, f32[128,3456]{1,0:T(8,128)} %fusion.40, ...), kind=kOutput, calls=%fused_computation.98 | convolution fusion | flops 510934784 | bytes 5900416 | tf_op jit(solution)/shard_map/dot_general | solution.py:412
  113.6 2.1 %scatter_custom_fusion = bf16[128,1152]{1,0:T(8,128)(2,1)} fusion(s32[128]{0:T(128)S(1)} %fusion.50, f32[128,1152]{1,0:T(8,128)S(1)} %get-tuple-element.25, bf16[1,128,1152]{2,1,0:T(8,128)(2,1)S(1)} %copy-done.3, f32[128]{0:T(128)S(1)} %get-tuple-element.26, f32[128]{0:T(128)S(1)} %get-tuple-element.27, f32[128]{0:T(128)S(1)} %add_rsqrt_fusion, ...), kind=kCustom, calls=%fused_computation.45 | custom fusion | flops 1622016 | bytes 1477122 | tf_op jit(solution)/shard_map/scatter | solution.py:425
  115.7 3.4 %all-to-all-start.3 = ((bf16[8,16,1152]{2,1,0:T(8,128)(2,1)}), bf16[8,16,1152]{2,1,0:T(8,128)(2,1)S(1)}, u32[]{:S(2)}, u32[]{:S(2)}) async-start(bf16[8,16,1152]{2,1,0:T(8,128)(2,1)} %bitcast.83), calls=%async_computation.3 | async-start | bytes 589824 | tf_op jit(solution)/shard_map/all_to_all | solution.py:426
  119.1 2.6 %convolution_convert_fusion = bf16[216,1152]{1,0:T(8,128)(2,1)S(1)} fusion(bf16[216,1024]{1,0:T(8,128)(2,1)} %bitcast.84, bf16[1024,2304]{1,0:T(8,128)(2,1)} %all-gather.2.cloned.1.call-done), kind=kOutput, calls=%fused_computation.5 | convolution fusion | flops 509856768 | bytes 3299328 | tf_op jit(solution)/shard_map/dot_general | solution.py:216
  121.7 2.3 %fusion.7 = bf16[72,1152]{1,0:T(8,128)(2,1)S(1)} fusion(bf16[1024,2304]{1,0:T(8,128)(2,1)} %all-gather.2.cloned.1.call-done, bf16[4,80,1024]{2,1,0:T(8,128)(2,1)} %get-tuple-element.20), kind=kOutput, calls=%fused_computation.16 | convolution fusion | flops 169952256 | bytes 2672640 | tf_op jit(solution)/shard_map/dot_general | solution.py:213
  124.0 0.9 pad_maximum_fusion
  124.9 4.5 %all-to-all-done.3 = bf16[8,16,1152]{2,1,0:T(8,128)(2,1)S(1)} async-done(((bf16[8,16,1152]{2,1,0:T(8,128)(2,1)}), bf16[8,16,1152]{2,1,0:T(8,128)(2,1)S(1)}, u32[]{:S(2)}, u32[]{:S(2)}) %all-to-all-start.3) | async-done | bytes 294944 | tf_op jit(solution)/shard_map/all_to_all | solution.py:426
  130.1 3.6 %all-to-all-start.4 = ((bf16[4,72,1152]{2,1,0:T(8,128)(2,1)}), bf16[4,72,1152]{2,1,0:T(8,128)(2,1)S(1)}, u32[]{:S(2)}, u32[]{:S(2)}) async-start(bf16[4,72,1152]{2,1,0:T(8,128)(2,1)} %bitcast.30), calls=%async_computation.4 | async-start | bytes 1327104 | tf_op jit(solution)/shard_map/all_to_all | solution.py:222
  133.8 2.6 %fusion.6 = bf16[1,128,1152]{2,1,0:T(8,128)(2,1)} fusion(bf16[576,128]{1,0:T(8,128)(2,1)S(1)} %bitcast.78, bf16[576,1152]{1,0:T(8,128)(2,1)} %param.24, f32[128,3456]{1,0:T(8,128)} %fusion.40, bf16[128,1152]{1,0:T(8,128)(2,1)S(1)} %gather_fusion.2, pred[128]{0:T(512)(128)(4,1)S(1)} %compare_and_fusion), kind=kOutput, calls=%fused_computation.15 | convolution fusion | flops 170606592 | bytes 2654336 | tf_op jit(solution)/shard_map/dot_general | solution.py:408
  136.4 2.2 %scatter_custom_fusion.1 = bf16[128,1152]{1,0:T(8,128)(2,1)} fusion(s32[128]{0:T(128)S(1)} %fusion.49, bf16[128,1152]{1,0:T(8,128)(2,1)} %bitcast.85, bf16[]{:T(256)} %constant.82.clone.1), kind=kCustom, calls=%fused_computation.55 | custom fusion | bytes 295424 | tf_op jit(solution)/shard_map/scatter | solution.py:427
  138.7 4.3 %all-to-all-done.4 = bf16[4,72,1152]{2,1,0:T(8,128)(2,1)S(1)} async-done(((bf16[4,72,1152]{2,1,0:T(8,128)(2,1)}), bf16[4,72,1152]{2,1,0:T(8,128)(2,1)S(1)}, u32[]{:S(2)}, u32[]{:S(2)}) %all-to-all-start.4) | async-done | bytes 663584 | tf_op jit(solution)/shard_map/all_to_all | solution.py:222
  143.7 42.5 %shard_map.139 = bf16[32,72,1152]{2,1,0:T(8,128)(2,1)} custom-call(bf16[72,1152]{1,0:T(8,128)(2,1)} %multiply_convert_fusion.share_ref), custom_call_target="tpu_custom_call" | custom-call | tf_op jit(solution)/shard_map/pallas_call | solution.py:166
  186.3 2.5 %slice.85 = bf16[8,72,1152]{2,1,0:T(8,128)(2,1)} slice(bf16[32,72,1152]{2,1,0:T(8,128)(2,1)} %shard_map.139), slice={[0:8], [0:72], [0:1152]} | slice | bytes 2654208 | tf_op jit(solution)/shard_map/slice | solution.py:229
  188.8 4.4 %slice.83 = bf16[24,72,1152]{2,1,0:T(8,128)(2,1)} slice(bf16[32,72,1152]{2,1,0:T(8,128)(2,1)} %shard_map.139), slice={[8:32], [0:72], [0:1152]} | slice | bytes 7962624 | tf_op jit(solution)/shard_map/slice | solution.py:228
  (58 shorter events, 5.8 us)
Async XLA Ops:
  7.2 11.0 %copy-start = (bf16[1001,1152]{1,0:T(8,128)(2,1)S(1)}, bf16[1001,1152]{1,0:T(8,128)(2,1)}, u32[]{:S(2)}) copy-start(bf16[1001,1152]{1,0:T(8,128)(2,1)} %param.21) | copy-start | bytes 6918916
  8.7 9.4 %copy-start.7 = (s32[1,16]{1,0:T(1,128)S(1)}, s32[1,16]{1,0:T(1,128)}, u32[]{:S(2)}) copy-start(s32[1,16]{1,0:T(1,128)} %param.19) | copy-start | bytes 196
  8.7 9.4 %copy-start.8 = (s32[1,16]{1,0:T(1,128)S(1)}, s32[1,16]{1,0:T(1,128)}, u32[]{:S(2)}) copy-start(s32[1,16]{1,0:T(1,128)} %param.20) | copy-start | bytes 196
  8.7 9.4 %copy-start.9 = (s32[1,1,128]{2,1,0:T(1,128)S(1)}, s32[1,1,128]{2,1,0:T(1,128)}, u32[]{:S(2)}) copy-start(s32[1,1,128]{2,1,0:T(1,128)} %param.17) | copy-start | bytes 1540
  11.6 16.8 %all-to-all-start = ((bf16[8,16,1152]{2,1,0:T(8,128)(2,1)}), bf16[8,16,1152]{2,1,0:T(8,128)(2,1)S(1)}, u32[]{:S(2)}, u32[]{:S(2)}) async-start(bf16[8,16,1152]{2,1,0:T(8,128)(2,1)} %bitcast.3), calls=%async_computation | async-start | bytes 589824 | tf_op jit(solution)/shard_map/all_to_all | solution.py:381
  18.0 101.1 %all-gather.2.cloned.1.call-start = ((), (), s32[]{:S(2)}) async-start(), calls=%async_computation.5 | async-start | bytes 5308416 | tf_op jit(solution)/shard_map/all_gather | solution.py:200
  18.7 4.5 %copy-start.5 = (s32[1,128]{1,0:T(1,128)S(1)}, s32[1,128]{1,0:T(1,128)}, u32[]{:S(2)}) copy-start(s32[1,128]{1,0:T(1,128)} %param.18) | copy-start | bytes 1540
  25.4 4.4 %copy-start.2 = (bf16[1,128,1152]{2,1,0:T(8,128)(2,1)S(1)}, bf16[1,128,1152]{2,1,0:T(8,128)(2,1)}, u32[]{:S(2)}) copy-start(bf16[1,128,1152]{2,1,0:T(8,128)(2,1)} %param.25) | copy-start | bytes 884740
  29.8 3.3 %copy-start.6 = (s32[4]{0:T(128)S(1)}, s32[4]{0:T(128)}, u32[]{:S(2)}) copy-start(s32[4]{0:T(128)} %constant.85.clone.1) | copy-start | bytes 52
  86.8 22.5 %all-to-all-start.2 = ((bf16[8,4,80,128]{3,2,1,0:T(8,128)(2,1)}), bf16[8,4,80,128]{3,2,1,0:T(8,128)(2,1)S(1)}, u32[]{:S(2)}, u32[]{:S(2)}) async-start(bf16[8,4,80,128]{3,2,1,0:T(8,128)(2,1)} %get-tuple-element.19), calls=%async_computation.2 | async-start | bytes 1310720 | tf_op jit(solution)/shard_map/all_to_all | solution.py:230
  109.4 0.8 copy-start.1
  110.3 3.3 %copy-start.3 = (bf16[1,128,1152]{2,1,0:T(8,128)(2,1)S(1)}, bf16[1,128,1152]{2,1,0:T(8,128)(2,1)}, u32[]{:S(2)}) copy-start(bf16[1,128,1152]{2,1,0:T(8,128)(2,1)} %param.25) | copy-start | bytes 884740
  115.7 13.8 %all-to-all-start.3 = ((bf16[8,16,1152]{2,1,0:T(8,128)(2,1)}), bf16[8,16,1152]{2,1,0:T(8,128)(2,1)S(1)}, u32[]{:S(2)}, u32[]{:S(2)}) async-start(bf16[8,16,1152]{2,1,0:T(8,128)(2,1)} %bitcast.83), calls=%async_computation.3 | async-start | bytes 589824 | tf_op jit(solution)/shard_map/all_to_all | solution.py:426
  124.0 9.8 %copy-start.10 = (s32[1,1,128]{2,1,0:T(1,128)S(1)}, s32[1,1,128]{2,1,0:T(1,128)}, u32[]{:S(2)}) copy-start(s32[1,1,128]{2,1,0:T(1,128)} %param.16) | copy-start | bytes 1540
  124.0 9.8 %slice-start = ((bf16[4,8,72,128]{3,2,0,1:T(8,128)(2,1)}), bf16[1,8,72,128]{3,2,0,1:T(8,128)(2,1)S(1)}, s32[]{:S(2)}) async-start(bf16[4,8,72,128]{3,2,0,1:T(8,128)(2,1)} %copy-done.1), calls=%async_computation.6 | async-start | bytes 294912 | tf_op jit(solution)/shard_map/slice | solution.py:232
  129.4 0.7 copy-start.4
  130.1 12.8 %all-to-all-start.4 = ((bf16[4,72,1152]{2,1,0:T(8,128)(2,1)}), bf16[4,72,1152]{2,1,0:T(8,128)(2,1)S(1)}, u32[]{:S(2)}, u32[]{:S(2)}) async-start(bf16[4,72,1152]{2,1,0:T(8,128)(2,1)} %bitcast.30), calls=%async_computation.4 | async-start | bytes 1327104 | tf_op jit(solution)/shard_map/all_to_all | solution.py:222
Sparse Core Ops, SparseCore 0:
  32.6 65.8 all-gather.1

commit v3 on v1

--- a/solution.py
+++ b/solution.py
@@ -87,8 +87,18 @@
             out_ref[s, part] = result[:, s * tokens : (s + 1) * tokens]
 
 
-def by_heads(hidden, attention_in, attention_out, branch, local_images, factor, scale):
-    tokens = hidden.shape[0]
+def by_heads(
+    hidden,
+    attention_in,
+    attention_out,
+    branch,
+    local_images,
+    factor,
+    scale,
+    gate,
+    gathered_cotangent,
+):
+    tokens, model_width = hidden.shape
     head_width = attention_out.shape[0] // HEADS
     padded = -(-(head_width + 8) // 16) * 16
     projected = lax.dot_general(
@@ -106,8 +116,15 @@
     sent = jnp.concatenate([parts, tail], axis=2)
     heads = lax.all_to_all(sent, "seq", split_axis=0, concat_axis=0, tiled=True)
     total_rows = heads.shape[0] * tokens
-    all_rows = lax.all_gather(
-        jnp.concatenate([hidden, branch], axis=1), "seq", axis=0, tiled=True
+    all_hidden = lax.all_gather(hidden, "seq", axis=0, tiled=True)
+    all_images = gathered_cotangent[:, model_width:]
+    image_order = jnp.arange(gate.shape[0], dtype=jnp.int32).astype(jnp.bfloat16)
+    one_hot = (all_images[:, :1] == image_order[None, :]).astype(jnp.float32)
+    all_gates = jnp.dot(
+        one_hot, gate, precision=lax.Precision.HIGHEST, preferred_element_type=jnp.float32
+    )
+    all_branch = (all_gates * gathered_cotangent[:, :model_width].astype(jnp.float32)).astype(
+        jnp.bfloat16
     )
     results, flat = pl.pallas_call(
         functools.partial(head_kernel, factor, math.gcd(total_rows, 256), head_width),
@@ -118,13 +135,12 @@
         in_specs=[pl.BlockSpec(memory_space=pltpu.VMEM)],
         out_specs=(pl.BlockSpec(memory_space=pltpu.VMEM),) * 2,
     )(heads)
-    model_width = hidden.shape[1]
     out_term = jnp.dot(
-        flat[0, :head_width], all_rows[:, model_width:], preferred_element_type=jnp.float32
+        flat[0, :head_width], all_branch, preferred_element_type=jnp.float32
     )
     in_term = jnp.dot(
         flat[1:, :head_width].reshape(3 * head_width, total_rows),
-        all_rows[:, :model_width],
+        all_hidden,
         preferred_element_type=jnp.float32,
     )
     terms = jnp.concatenate([out_term, in_term], axis=0).astype(jnp.bfloat16)
@@ -286,6 +302,15 @@
     inner_width = attention_out.shape[0]
     head_width = inner_width // HEADS
     factor = head_width ** (-0.5)
+    split_heads = shard_count == HEADS and lax.axis_size("grp") == 4
+    if split_heads:
+        image_columns = jnp.broadcast_to(segment_ids[0][:, None], (tokens, 128))
+        gathered_cotangent = lax.all_gather(
+            jnp.concatenate([cotangent[0], image_columns.astype(jnp.bfloat16)], axis=1),
+            "seq",
+            axis=0,
+            tiled=True,
+        )
     outgoing = jnp.take(owned_patches[0], send_rows[0, 0], axis=0)
     incoming = lax.all_to_all(outgoing, "seq", split_axis=0, concat_axis=0, tiled=True)
     packed = jnp.take(incoming, receive_slot[0, 0], axis=0)
@@ -310,10 +335,12 @@
     upstream = cotangent[0].astype(jnp.float32)
     branch = (gate_rows * upstream).astype(jnp.bfloat16)
     norm_factor = (lax.axis_size("grp") * shard_count * tokens) ** (-0.5)
-    split = by_heads if shard_count == HEADS and lax.axis_size("grp") == 4 else by_tokens
-    attended, input_cotangent, gradient_in, gradient_out = split(
-        hidden, attention_in, attention_out, branch, local_images, factor, norm_factor
-    )
+    common = (hidden, attention_in, attention_out, branch, local_images, factor, norm_factor)
+    if split_heads:
+        results = by_heads(*common, modulation[:, 2 * model_width :], gathered_cotangent)
+    else:
+        results = by_tokens(*common)
+    attended, input_cotangent, gradient_in, gradient_out = results
     projected = lax.dot_general(
         attended, attention_out, (((0,), (0,)), ((), ())), preferred_element_type=jnp.float32
     )

time: 197 us -> 197 us (level)
  blocking collectives: 52.8 us -> 11.7 us
  waiting for transfers between devices: 59.8 us -> 85.9 us
  starting transfers between devices: 13.6 us -> 19.9 us
  matrix products: 22.6 us -> 26.9 us
  other arithmetic: 9.69 us -> 12 us
    all_to_all x1 -> x0, blocking collectives: 38.6 us -> none  [by_heads(): heads = lax.all_to_all(sent, 'seq', split_axis=0, concat_axis=0, tiled=True)]
    all_to_all x0 -> x1, waiting for transfers between devices: none -> 27.7 us  [by_heads(): heads = lax.all_to_all(sent, 'seq', split_axis=0, concat_axis=0, tiled=True)]
    all_gather x1 -> x2, waiting for transfers between devices: 8.93 us -> 0.02 us  [the longest x1 0.02 us: by_heads(): all_hidden = lax.all_gather(hidden, 'seq', axis=0, tiled=True)]
    all_to_all x1, waiting for transfers between devices: 3.04 us -> 9.06 us  [shards(): lax.all_to_all(outgoing, 'seq', split_axis=0, concat_axis=0, tiled=True)]
    all_to_all x0 -> x1, starting transfers between devices: none -> 4.69 us  [by_heads(): heads = lax.all_to_all(sent, 'seq', split_axis=0, concat_axis=0, tiled=True)]
    dot_general x2 -> x3, matrix products: 4.71 us -> 7.86 us  [the longest x1 3.84 us: by_heads(): jnp.dot(one_hot, gate, precision=lax.Precision.HIGHEST, preferred_element...]
    all_to_all x1, blocking collectives: 14.2 us -> 11.7 us  [by_heads(): lax.all_to_all(terms.reshape(4, head_width, model_width), 'grp', split_ax...]
  transfers between devices with their start and end apart: 5 -> 7, of which waited for: 5 -> 5; matrix products, arithmetic and copies ran while one was open for 13% -> 22% of each run, Pallas kernels for 4% -> 4%
where the time goes in v3:
time: 197 us; the launch traced here: 196 us
  waiting for transfers between devices  85.9 us (44%)
  matrix products  26.9 us (14%)
  starting transfers between devices  19.9 us (10%)
  local copies, waits for them, and re-layouts  17.6 us (9%)
  between operations  14.7 us (7%)
  other arithmetic  12 us (6%)
  blocking collectives  11.7 us (6%)
  Pallas kernels  7.25 us (4%)
    all_to_all x1, waiting for transfers between devices, by_heads(): heads = lax.all_to_all(sent, 'seq', split_axis=0, concat_axis=0, tiled=True)  27.7 us
    all_to_all x1, waiting for transfers between devices, by_heads(): lax.all_to_all(results, 'seq', split_axis=0, concat_axis=0, tiled=True)  21.8 us
    all_gather x1, waiting for transfers between devices, by_heads(): joined = lax.all_gather(share, ('grp', 'seq'), axis=0, tiled=True)  19.3 us
    all_to_all x1, blocking collectives, by_heads(): lax.all_to_all(terms.reshape(4, head_width, model_width), 'grp', split_ax...  11.7 us
    all_to_all x1, waiting for transfers between devices, shards(): lax.all_to_all(outgoing, 'seq', split_axis=0, concat_axis=0, tiled=True)  9.06 us
    all_to_all x1, waiting for transfers between devices, shards(): lax.all_to_all(back_order, 'seq', split_axis=0, concat_axis=0, tiled=True)  7.95 us
    pallas_call x1, Pallas kernels, by_heads(): pl.pallas_call(functools.partial(head_kernel, factor, math.gcd(total_rows...  7.25 us
    all_to_all x1, starting transfers between devices, shards(): lax.all_to_all(outgoing, 'seq', split_axis=0, concat_axis=0, tiled=True)  6.36 us
  transfers between devices with their start and end apart: 7, of which 5 were waited for; matrix products, arithmetic and copies ran while one was open for 22% of the time, Pallas kernels for 4%

profile of v3, /device:TPU:0, one launch (start us, length us, event | category | flops | bytes accessed | tf_op | source)
XLA Modules:
  0.0 195.9 jit_solution(10758302270322994363)
XLA Ops:
  8.2 1.7 pad_maximum_fusion.3
  10.6 0.9 gather_fusion.1
  12.4 6.4 %all-to-all-start = ((bf16[8,16,1152]{2,1,0:T(8,128)(2,1)}), bf16[8,16,1152]{2,1,0:T(8,128)(2,1)S(1)}, u32[]{:S(2)}, u32[]{:S(2)}) async-start(bf16[8,16,1152]{2,1,0:T(8,128)(2,1)} %bitcast.3), calls=%async_computation | async-start | bytes 589824 | tf_op jit(solution)/shard_map/all_to_all | solution.py:315
  19.5 4.8 %fusion.40 = f32[16,3456]{1,0:T(8,128)S(1)} fusion(bf16[1152,3456]{1,0:T(8,128)(2,1)} %param.22, bf16[16,1152]{1,0:T(8,128)(2,1)S(1)} %gather_fusion, pred[16]{0:T(512)(128)(4,1)S(1)} %compare_and_fusion.2), kind=kOutput, calls=%fused_computation.70 | convolution fusion | flops 127531008 | bytes 8220688 | tf_op jit(solution)/shard_map/dot_general | solution.py:320
  24.3 2.1 %fusion.39 = f32[128,3456]{1,0:T(8,128)} fusion(f32[16,3456]{1,0:T(8,128)S(1)} %fusion.40, s32[128]{0:T(128)S(1)} %bitcast.87), kind=kOutput, calls=%fused_computation.69 | convolution fusion | flops 84936704 | bytes 1991168 | tf_op jit(solution)/shard_map/dot_general | solution.py:326
  26.4 9.1 %all-to-all-done = bf16[8,16,1152]{2,1,0:T(8,128)(2,1)S(1)} async-done(((bf16[8,16,1152]{2,1,0:T(8,128)(2,1)}), bf16[8,16,1152]{2,1,0:T(8,128)(2,1)S(1)}, u32[]{:S(2)}, u32[]{:S(2)}) %all-to-all-start) | async-done | bytes 294944 | tf_op jit(solution)/shard_map/all_to_all | solution.py:315
  35.5 0.9 gather_fusion.2
  36.8 2.2 %fusion.12 = bf16[128,1152]{1,0:T(8,128)(2,1)} fusion(f32[128,3456]{1,0:T(8,128)} %fusion.39, f32[128]{0:T(128)S(1)} %add_rsqrt_fusion, f32[128]{0:T(128)S(1)} %broadcast_multiply_fusion.3, bf16[128,1152]{1,0:T(8,128)(2,1)S(1)} %gather_fusion.2, pred[128]{0:T(512)(128)(4,1)S(1)} %compare_and_fusion), kind=kLoop, calls=%fused_computation.32 | loop fusion | flops 1179648 | bytes 1770624 | tf_op jit(solution)/shard_map/convert_element_type | solution.py:334
  42.0 2.0 %fusion.5 = bf16[576,128]{1,0:T(8,128)(2,1)S(1)} fusion(bf16[576,1152]{1,0:T(8,128)(2,1)} %param.24, f32[128,3456]{1,0:T(8,128)} %fusion.39, bf16[1,128,1152]{2,1,0:T(8,128)(2,1)S(1)} %copy-done.2), kind=kOutput, calls=%fused_computation.19 | convolution fusion | flops 170385408 | bytes 2359296 | tf_op jit(solution)/shard_map/dot_general | solution.py:107
  44.0 3.4 %fusion.3 = bf16[1728,128]{1,0:T(8,128)(2,1)S(1)} fusion(bf16[128,1152]{1,0:T(8,128)(2,1)S(1)} %copy-done.3, bf16[1152,1728]{0,1:T(8,128)(2,1)} %param.23), kind=kOutput, calls=%fused_computation.14 | convolution fusion | flops 509829120 | bytes 4718592 | tf_op jit(solution)/shard_map/dot_general | solution.py:104
  47.5 0.9 pad_maximum_fusion.1
  48.4 4.7 %all-to-all-start.1 = ((bf16[8,4,80,128]{3,2,1,0:T(8,128)(2,1)}), bf16[8,4,80,128]{3,2,1,0:T(8,128)(2,1)}, u32[]{:S(2)}, u32[]{:S(2)}) async-start(bf16[8,4,80,128]{3,2,1,0:T(8,128)(2,1)} %pad_maximum_fusion.1), calls=%async_computation.1 | async-start | bytes 1310720 | tf_op jit(solution)/shard_map/all_to_all | solution.py:117
  53.3 27.7 %all-to-all-done.1.packed_ref = bf16[8,4,80,128]{3,2,1,0:T(8,128)(2,1)} async-done(((bf16[8,4,80,128]{3,2,1,0:T(8,128)(2,1)}), bf16[8,4,80,128]{3,2,1,0:T(8,128)(2,1)}, u32[]{:S(2)}, u32[]{:S(2)}) %all-to-all-start.1) | async-done | bytes 655392 | tf_op jit(solution)/shard_map/all_to_all | solution.py:117
  81.0 7.2 %shard_map.138 = (bf16[8,4,80,128]{3,2,1,0:T(8,128)(2,1)}, bf16[4,80,1024]{2,1,0:T(8,128)(2,1)}) custom-call(bf16[8,4,80,128]{3,2,1,0:T(8,128)(2,1)} %all-to-all-done.1.packed_ref), custom_call_target="tpu_custom_call" | custom-call | tf_op jit(solution)/shard_map/pallas_call | solution.py:129
  88.3 1.8 slice.82
  90.1 1.1 slice_reduce_fusion
  91.2 3.8 %fusion = bf16[1024,1152]{1,0:T(8,128)(2,1)S(1)} fusion(bf16[1024,1280]{1,0:T(8,128)(2,1)} %all-gather.4.cloned.1.call-done, bf16[16]{0:T(256)(128)(2,1)S(1)} %iota_convert_fusion, bf16[1024]{0:T(1024)(128)(2,1)S(1)} %slice_reduce_fusion, f32[16,3456]{1,0:T(8,128)S(1)} %fusion.40), kind=kOutput, calls=%fused_computation.7 | convolution fusion | flops 230047744 | bytes 4794880 | tf_op jit(solution)/shard_map/dot_general | solution.py:123
  95.0 1.5 convolution_convert_fusion.2
  96.5 2.6 %convolution_convert_fusion = bf16[216,1152]{1,0:T(8,128)(2,1)S(1)} fusion(bf16[216,1024]{1,0:T(8,128)(2,1)} %bitcast.84, bf16[1024,1152]{1,0:T(8,128)(2,1)} %all-gather.6.cloned.1.call-done), kind=kOutput, calls=%fused_computation.8 | convolution fusion | flops 509856768 | bytes 3299328 | tf_op jit(solution)/shard_map/dot_general | solution.py:141
  99.1 11.7 %all_to_all.39 = bf16[4,72,1152]{2,1,0:T(8,128)(2,1)S(1)} all-to-all(bf16[4,72,1152]{2,1,0:T(8,128)(2,1)S(1)} %bitcast.79), channel_id=1, replica_groups=mesh['grp'=4,'seq'=8] {'grp'}, dimensions={0} | all-to-all | bytes 1327104 | tf_op jit(solution)/shard_map/all_to_all | solution.py:147
  111.6 5.1 %all-to-all-start.2 = ((bf16[8,4,80,128]{3,2,1,0:T(8,128)(2,1)}), bf16[8,4,80,128]{3,2,1,0:T(8,128)(2,1)}, u32[]{:S(2)}, u32[]{:S(2)}) async-start(bf16[8,4,80,128]{3,2,1,0:T(8,128)(2,1)} %get-tuple-element.19), calls=%async_computation.2 | async-start | bytes 1310720 | tf_op jit(solution)/shard_map/all_to_all | solution.py:155
  116.7 21.8 %all-to-all-done.2 = bf16[8,4,80,128]{3,2,1,0:T(8,128)(2,1)} async-done(((bf16[8,4,80,128]{3,2,1,0:T(8,128)(2,1)}), bf16[8,4,80,128]{3,2,1,0:T(8,128)(2,1)}, u32[]{:S(2)}, u32[]{:S(2)}) %all-to-all-start.2) | async-done | bytes 655392 | tf_op jit(solution)/shard_map/all_to_all | solution.py:155
  138.5 1.1 slice_bitcast_fusion.1
  140.6 4.1 %fusion.54 = (f32[128]{0:T(128)S(1)}, f32[128]{0:T(128)S(1)}, f32[128,1152]{1,0:T(8,128)}) fusion(f32[128]{0:T(128)S(1)} %add_rsqrt_fusion, f32[128]{0:T(128)S(1)} %broadcast_multiply_fusion.3, bf16[128,1152]{1,0:T(8,128)(2,1)S(1)} %gather_fusion.2, pred[128]{0:T(512)(128)(4,1)S(1)} %compare_and_fusion, f32[128,3456]{1,0:T(8,128)} %fusion.39, ...), kind=kOutput, calls=%fused_computation.105 | convolution fusion | flops 510934784 | bytes 5900416 | tf_op jit(solution)/shard_map/dot_general | solution.py:348
  144.7 2.6 %scatter_custom_fusion = bf16[128,1152]{1,0:T(8,128)(2,1)} fusion(s32[128]{0:T(128)S(1)} %fusion.49, f32[128,1152]{1,0:T(8,128)} %get-tuple-element.23, f32[128]{0:T(128)S(1)} %get-tuple-element.24, f32[128]{0:T(128)S(1)} %get-tuple-element.25, f32[128]{0:T(128)S(1)} %add_rsqrt_fusion, f32[128]{0:T(128)S(1)} %broadcast_multiply_fusion.3, ...), kind=kCustom, calls=%fused_computation.46 | custom fusion | flops 1622016 | bytes 1477122 | tf_op jit(solution)/shard_map/scatter | solution.py:361
  147.3 3.4 %all-to-all-start.3 = ((bf16[8,16,1152]{2,1,0:T(8,128)(2,1)}), bf16[8,16,1152]{2,1,0:T(8,128)(2,1)S(1)}, u32[]{:S(2)}, u32[]{:S(2)}) async-start(bf16[8,16,1152]{2,1,0:T(8,128)(2,1)} %bitcast.24), calls=%async_computation.3 | async-start | bytes 589824 | tf_op jit(solution)/shard_map/all_to_all | solution.py:362
  150.8 2.6 %fusion.4 = bf16[1,128,1152]{2,1,0:T(8,128)(2,1)} fusion(bf16[576,128]{1,0:T(8,128)(2,1)S(1)} %bitcast.80, bf16[576,1152]{1,0:T(8,128)(2,1)} %param.24, f32[128,3456]{1,0:T(8,128)} %fusion.39, bf16[128,1152]{1,0:T(8,128)(2,1)S(1)} %gather_fusion.2, pred[128]{0:T(512)(128)(4,1)S(1)} %compare_and_fusion), kind=kOutput, calls=%fused_computation.15 | convolution fusion | flops 170606592 | bytes 2654336 | tf_op jit(solution)/shard_map/dot_general | solution.py:344
  153.4 8.0 %all-to-all-done.3 = bf16[8,16,1152]{2,1,0:T(8,128)(2,1)S(1)} async-done(((bf16[8,16,1152]{2,1,0:T(8,128)(2,1)}), bf16[8,16,1152]{2,1,0:T(8,128)(2,1)S(1)}, u32[]{:S(2)}, u32[]{:S(2)}) %all-to-all-start.3) | async-done | bytes 294944 | tf_op jit(solution)/shard_map/all_to_all | solution.py:362
  161.4 1.8 scatter_custom_fusion.1
  163.2 19.3 %all-gather.8.cloned.1.call-done = bf16[2304,1152]{1,0:T(8,128)(2,1)} async-done(((bf16[72,1152]{1,0:T(8,128)(2,1)}), bf16[2304,1152]{1,0:T(8,128)(2,1)}) %all-gather.8.cloned.1.call-update) | async-done | bytes 5308432 | tf_op jit(solution)/shard_map/all_gather | solution.py:151
  182.5 2.5 %slice.101 = bf16[576,1152]{1,0:T(8,128)(2,1)} slice(bf16[2304,1152]{1,0:T(8,128)(2,1)} %all-gather.8.cloned.1.call-done), slice={[0:576], [0:1152]} | slice | bytes 2654208 | tf_op jit(solution)/shard_map/slice | solution.py:154
  185.0 4.4 %slice_bitcast_fusion = bf16[1152,1728]{0,1:T(8,128)(2,1)} fusion(bf16[2304,1152]{1,0:T(8,128)(2,1)} %all-gather.8.cloned.1.call-done), kind=kLoop, calls=%fused_computation.6 | loop fusion | bytes 7962624 | tf_op jit(solution)/shard_map/transpose | solution.py:153
  (67 shorter events, 8.0 us)
Async XLA Ops:
  7.2 11.7 %copy-start = (bf16[1001,1152]{1,0:T(8,128)(2,1)S(1)}, bf16[1001,1152]{1,0:T(8,128)(2,1)}, u32[]{:S(2)}) copy-start(bf16[1001,1152]{1,0:T(8,128)(2,1)} %param.21) | copy-start | bytes 6918916
  7.2 4.4 %copy-start.10 = (s32[1,1,128]{2,1,0:T(1,128)S(1)}, s32[1,1,128]{2,1,0:T(1,128)}, u32[]{:S(2)}) copy-start(s32[1,1,128]{2,1,0:T(1,128)} %param.16) | copy-start | bytes 1540
  7.2 3.4 %copy-start.1 = (bf16[1,128,1152]{2,1,0:T(8,128)(2,1)S(1)}, bf16[1,128,1152]{2,1,0:T(8,128)(2,1)}, u32[]{:S(2)}) copy-start(bf16[1,128,1152]{2,1,0:T(8,128)(2,1)} %param.15) | copy-start | bytes 884740
  7.2 82.9 %all-gather.4.cloned.1.call-start = ((), (), s32[]{:S(2)}) async-start(), calls=%async_computation.5 | async-start | bytes 2949120 | tf_op jit(solution)/shard_map/all_gather | solution.py:308
  8.2 10.6 %copy-start.7 = (s32[1,16]{1,0:T(1,128)S(1)}, s32[1,16]{1,0:T(1,128)}, u32[]{:S(2)}) copy-start(s32[1,16]{1,0:T(1,128)} %param.19) | copy-start | bytes 196
  8.2 10.6 %copy-start.8 = (s32[1,16]{1,0:T(1,128)S(1)}, s32[1,16]{1,0:T(1,128)}, u32[]{:S(2)}) copy-start(s32[1,16]{1,0:T(1,128)} %param.20) | copy-start | bytes 196
  9.9 9.5 %copy-start.9 = (s32[1,1,128]{2,1,0:T(1,128)S(1)}, s32[1,1,128]{2,1,0:T(1,128)}, u32[]{:S(2)}) copy-start(s32[1,1,128]{2,1,0:T(1,128)} %param.17) | copy-start | bytes 1540
  12.4 23.1 %all-to-all-start = ((bf16[8,16,1152]{2,1,0:T(8,128)(2,1)}), bf16[8,16,1152]{2,1,0:T(8,128)(2,1)S(1)}, u32[]{:S(2)}, u32[]{:S(2)}) async-start(bf16[8,16,1152]{2,1,0:T(8,128)(2,1)} %bitcast.3), calls=%async_computation | async-start | bytes 589824 | tf_op jit(solution)/shard_map/all_to_all | solution.py:315
  18.7 77.8 %all-gather.6.cloned.1.call-start = ((), (), s32[]{:S(2)}) async-start(), calls=%async_computation.6 | async-start | bytes 2654208 | tf_op jit(solution)/shard_map/all_gather | solution.py:119
  19.5 4.8 %copy-start.5 = (s32[1,128]{1,0:T(1,128)S(1)}, s32[1,128]{1,0:T(1,128)}, u32[]{:S(2)}) copy-start(s32[1,128]{1,0:T(1,128)} %param.18) | copy-start | bytes 1540
  35.4 4.3 %copy-start.6 = (s32[4]{0:T(128)S(1)}, s32[4]{0:T(128)}, u32[]{:S(2)}) copy-start(s32[4]{0:T(128)} %constant.85.clone.1) | copy-start | bytes 52
  35.5 6.5 %copy-start.2 = (bf16[1,128,1152]{2,1,0:T(8,128)(2,1)S(1)}, bf16[1,128,1152]{2,1,0:T(8,128)(2,1)}, u32[]{:S(2)}) copy-start(bf16[1,128,1152]{2,1,0:T(8,128)(2,1)} %param.25) | copy-start | bytes 884740
  39.1 4.9 %copy-start.3 = (bf16[128,1152]{1,0:T(8,128)(2,1)S(1)}, bf16[128,1152]{1,0:T(8,128)(2,1)}, u32[]{:S(2)}) copy-start(bf16[128,1152]{1,0:T(8,128)(2,1)} %fusion.12) | copy-start | bytes 884740
  48.4 32.6 %all-to-all-start.1 = ((bf16[8,4,80,128]{3,2,1,0:T(8,128)(2,1)}), bf16[8,4,80,128]{3,2,1,0:T(8,128)(2,1)}, u32[]{:S(2)}, u32[]{:S(2)}) async-start(bf16[8,4,80,128]{3,2,1,0:T(8,128)(2,1)} %pad_maximum_fusion.1), calls=%async_computation.1 | async-start | bytes 1310720 | tf_op jit(solution)/shard_map/all_to_all | solution.py:117
  53.1 129.4 %all-gather.8.cloned.1.call-start = ((), (), s32[]{:S(2)}) async-start(), calls=%async_computation.7 | async-start | bytes 5474304 | tf_op jit(solution)/shard_map/all_gather | solution.py:151
  111.6 26.9 %all-to-all-start.2 = ((bf16[8,4,80,128]{3,2,1,0:T(8,128)(2,1)}), bf16[8,4,80,128]{3,2,1,0:T(8,128)(2,1)}, u32[]{:S(2)}, u32[]{:S(2)}) async-start(bf16[8,4,80,128]{3,2,1,0:T(8,128)(2,1)} %get-tuple-element.19), calls=%async_computation.2 | async-start | bytes 1310720 | tf_op jit(solution)/shard_map/all_to_all | solution.py:155
  139.7 0.8 copy-start.4
  144.7 6.1 %slice-start = ((bf16[4,8,72,128]{3,2,0,1:T(8,128)(2,1)}), bf16[1,8,72,128]{3,2,0,1:T(8,128)(2,1)S(1)}, s32[]{:S(2)}) async-start(bf16[4,8,72,128]{3,2,0,1:T(8,128)(2,1)} %copy-done.4), calls=%async_computation.8 | async-start | bytes 294912 | tf_op jit(solution)/shard_map/slice | solution.py:157
  147.3 14.1 %all-to-all-start.3 = ((bf16[8,16,1152]{2,1,0:T(8,128)(2,1)}), bf16[8,16,1152]{2,1,0:T(8,128)(2,1)S(1)}, u32[]{:S(2)}, u32[]{:S(2)}) async-start(bf16[8,16,1152]{2,1,0:T(8,128)(2,1)} %bitcast.24), calls=%async_computation.3 | async-start | bytes 589824 | tf_op jit(solution)/shard_map/all_to_all | solution.py:362
Sparse Core Ops, SparseCore 0:
  10.1 41.6 all-gather.3
  53.9 37.7 all-gather.5
  111.8 70.7 all-gather.7

commit v4 on v2

--- a/solution.py
+++ b/solution.py
@@ -178,8 +178,18 @@
     return gathered.reshape(count * share.shape[0], share.shape[1])
 
 
-def by_heads(hidden, attention_in, attention_out, branch, local_images, factor, scale):
-    tokens = hidden.shape[0]
+def by_heads(
+    hidden,
+    attention_in,
+    attention_out,
+    branch,
+    local_images,
+    factor,
+    scale,
+    gate,
+    gathered_cotangent,
+):
+    tokens, model_width = hidden.shape
     head_width = attention_out.shape[0] // HEADS
     padded = -(-(head_width + 8) // 16) * 16
     projected = lax.dot_general(
@@ -197,8 +207,15 @@
     sent = jnp.concatenate([parts, tail], axis=2)
     heads = lax.all_to_all(sent, "seq", split_axis=0, concat_axis=0, tiled=True)
     total_rows = heads.shape[0] * tokens
-    all_rows = lax.all_gather(
-        jnp.concatenate([hidden, branch], axis=1), "seq", axis=0, tiled=True
+    all_hidden = lax.all_gather(hidden, "seq", axis=0, tiled=True)
+    all_images = gathered_cotangent[:, model_width:]
+    image_order = jnp.arange(gate.shape[0], dtype=jnp.int32).astype(jnp.bfloat16)
+    one_hot = (all_images[:, :1] == image_order[None, :]).astype(jnp.float32)
+    all_gates = jnp.dot(
+        one_hot, gate, precision=lax.Precision.HIGHEST, preferred_element_type=jnp.float32
+    )
+    all_branch = (all_gates * gathered_cotangent[:, :model_width].astype(jnp.float32)).astype(
+        jnp.bfloat16
     )
     results, flat = pl.pallas_call(
         functools.partial(head_kernel, factor, math.gcd(total_rows, 256), head_width),
@@ -209,13 +226,12 @@
         in_specs=[pl.BlockSpec(memory_space=pltpu.VMEM)],
         out_specs=(pl.BlockSpec(memory_space=pltpu.VMEM),) * 2,
     )(heads)
-    model_width = hidden.shape[1]
     out_term = jnp.dot(
-        flat[0, :head_width], all_rows[:, model_width:], preferred_element_type=jnp.float32
+        flat[0, :head_width], all_branch, preferred_element_type=jnp.float32
     )
     in_term = jnp.dot(
         flat[1:, :head_width].reshape(3 * head_width, total_rows),
-        all_rows[:, :model_width],
+        all_hidden,
         preferred_element_type=jnp.float32,
     )
     terms = jnp.concatenate([out_term, in_term], axis=0).astype(jnp.bfloat16)
@@ -377,6 +393,15 @@
     inner_width = attention_out.shape[0]
     head_width = inner_width // HEADS
     factor = head_width ** (-0.5)
+    split_heads = shard_count == HEADS and lax.axis_size("grp") == 4
+    if split_heads:
+        image_columns = jnp.broadcast_to(segment_ids[0][:, None], (tokens, 128))
+        gathered_cotangent = lax.all_gather(
+            jnp.concatenate([cotangent[0], image_columns.astype(jnp.bfloat16)], axis=1),
+            "seq",
+            axis=0,
+            tiled=True,
+        )
     outgoing = jnp.take(owned_patches[0], send_rows[0, 0], axis=0)
     incoming = lax.all_to_all(outgoing, "seq", split_axis=0, concat_axis=0, tiled=True)
     packed = jnp.take(incoming, receive_slot[0, 0], axis=0)
@@ -401,10 +426,12 @@
     upstream = cotangent[0].astype(jnp.float32)
     branch = (gate_rows * upstream).astype(jnp.bfloat16)
     norm_factor = (lax.axis_size("grp") * shard_count * tokens) ** (-0.5)
-    split = by_heads if shard_count == HEADS and lax.axis_size("grp") == 4 else by_tokens
-    attended, input_cotangent, gradient_in, gradient_out = split(
-        hidden, attention_in, attention_out, branch, local_images, factor, norm_factor
-    )
+    common = (hidden, attention_in, attention_out, branch, local_images, factor, norm_factor)
+    if split_heads:
+        results = by_heads(*common, modulation[:, 2 * model_width :], gathered_cotangent)
+    else:
+        results = by_tokens(*common)
+    attended, input_cotangent, gradient_in, gradient_out = results
     projected = lax.dot_general(
         attended, attention_out, (((0,), (0,)), ((), ())), preferred_element_type=jnp.float32
     )

time: 201 us -> 196 us (0.975); the launches traced: 200 us -> 192 us
  blocking collectives: 38.6 us -> 27 us
  matrix products: 22.8 us -> 27.4 us
  waiting for transfers between devices: 28.8 us -> 24.8 us
    all_to_all x1, blocking collectives: 38.6 us -> 27 us  [by_heads(): heads = lax.all_to_all(sent, 'seq', split_axis=0, concat_axis=0, tiled=True)]
    all_to_all x1, waiting for transfers between devices: 4.53 us -> 0.55 us  [shards(): lax.all_to_all(back_order, 'seq', split_axis=0, concat_axis=0, tiled=True)]
    dot_general x2 -> x3, matrix products: 4.85 us -> 7.76 us  [the longest x1 3.84 us: by_heads(): jnp.dot(one_hot, gate, precision=lax.Precision.HIGHEST, preferred_element...]
  transfers between devices with their start and end apart: 5 -> 6, of which waited for: 4 -> 4; matrix products, arithmetic and copies ran while one was open for 16% -> 24% of each run, Pallas kernels for 4% -> 4%
where the time goes in v4:
time: 196 us; the launch traced here: 192 us
  Pallas kernels  49.4 us (25%)
  matrix products  27.4 us (14%)
  blocking collectives  27 us (14%)
  waiting for transfers between devices  24.8 us (13%)
  starting transfers between devices  18.6 us (9%)
  local copies, waits for them, and re-layouts  18.1 us (9%)
  between operations  15.1 us (8%)
  other arithmetic  12 us (6%)
    pallas_call x1, Pallas kernels, gather_all(): pl.pallas_call(gather_kernel, out_shape=jax.ShapeDtypeStruct((count, *sha...  42.1 us
    all_to_all x1, blocking collectives, by_heads(): heads = lax.all_to_all(sent, 'seq', split_axis=0, concat_axis=0, tiled=True)  27 us
    all_to_all x1, waiting for transfers between devices, by_heads(): lax.all_to_all(results, 'seq', split_axis=0, concat_axis=0, tiled=True)  16.1 us
    pallas_call x1, Pallas kernels, by_heads(): pl.pallas_call(functools.partial(head_kernel, factor, math.gcd(total_rows...  7.29 us
    all_to_all x1, starting transfers between devices, shards(): lax.all_to_all(outgoing, 'seq', split_axis=0, concat_axis=0, tiled=True)  6.35 us
    dot_general x1, matrix products, shards(): jnp.dot(activated, modulation_weight, preferred_element_type=jnp.float32)  4.71 us
    all_to_all x1, waiting for transfers between devices, by_heads(): lax.all_to_all(terms.reshape(4, head_width, model_width), 'grp', split_ax...  4.58 us
    all_to_all x1, starting transfers between devices, by_heads(): lax.all_to_all(results, 'seq', split_axis=0, concat_axis=0, tiled=True)  4.38 us
  transfers between devices with their start and end apart: 6, of which 4 were waited for; matrix products, arithmetic and copies ran while one was open for 24% of the time, Pallas kernels for 4%

profile of v4, /device:TPU:0, one launch (start us, length us, event | category | flops | bytes accessed | tf_op | source)
XLA Modules:
  0.0 192.3 jit_solution(15402915480111095553)
XLA Ops:
  7.2 0.8 bitcast_convert_fusion
  8.2 1.7 pad_maximum_fusion.3
  10.6 0.9 gather_fusion.1
  12.4 6.4 %all-to-all-start = ((bf16[8,16,1152]{2,1,0:T(8,128)(2,1)}), bf16[8,16,1152]{2,1,0:T(8,128)(2,1)S(1)}, u32[]{:S(2)}, u32[]{:S(2)}) async-start(bf16[8,16,1152]{2,1,0:T(8,128)(2,1)} %bitcast.3), calls=%async_computation | async-start | bytes 589824 | tf_op jit(solution)/shard_map/all_to_all | solution.py:406
  20.2 4.7 %fusion.40 = f32[16,3456]{1,0:T(8,128)S(1)} fusion(bf16[1152,3456]{1,0:T(8,128)(2,1)} %param.22, bf16[16,1152]{1,0:T(8,128)(2,1)S(1)} %gather_fusion, pred[16]{0:T(512)(128)(4,1)S(1)} %compare_and_fusion.2), kind=kOutput, calls=%fused_computation.69 | convolution fusion | flops 127531008 | bytes 8220688 | tf_op jit(solution)/shard_map/dot_general | solution.py:411
  24.9 2.1 %fusion.39 = f32[128,3456]{1,0:T(8,128)} fusion(f32[16,3456]{1,0:T(8,128)S(1)} %fusion.40, s32[128]{0:T(128)S(1)} %bitcast.89), kind=kOutput, calls=%fused_computation.68 | convolution fusion | flops 84936704 | bytes 1991168 | tf_op jit(solution)/shard_map/dot_general | solution.py:417
  29.3 2.7 %fusion.5 = bf16[576,128]{1,0:T(8,128)(2,1)} fusion(bf16[576,1152]{1,0:T(8,128)(2,1)} %param.24, f32[128,3456]{1,0:T(8,128)} %fusion.39, bf16[1,128,1152]{2,1,0:T(8,128)(2,1)S(1)} %copy-done.2), kind=kOutput, calls=%fused_computation.18 | convolution fusion | flops 170385408 | bytes 2359296 | tf_op jit(solution)/shard_map/dot_general | solution.py:198
  32.0 3.5 %all-to-all-done = bf16[8,16,1152]{2,1,0:T(8,128)(2,1)S(1)} async-done(((bf16[8,16,1152]{2,1,0:T(8,128)(2,1)}), bf16[8,16,1152]{2,1,0:T(8,128)(2,1)S(1)}, u32[]{:S(2)}, u32[]{:S(2)}) %all-to-all-start) | async-done | bytes 294944 | tf_op jit(solution)/shard_map/all_to_all | solution.py:406
  35.4 0.9 gather_fusion.2
  36.8 2.2 %fusion.12 = bf16[128,1152]{1,0:T(8,128)(2,1)} fusion(f32[128,3456]{1,0:T(8,128)} %fusion.39, f32[128]{0:T(128)S(1)} %add_rsqrt_fusion, f32[128]{0:T(128)S(1)} %broadcast_multiply_fusion.3, bf16[128,1152]{1,0:T(8,128)(2,1)S(1)} %gather_fusion.2, pred[128]{0:T(512)(128)(4,1)S(1)} %compare_and_fusion), kind=kLoop, calls=%fused_computation.31 | loop fusion | flops 1179648 | bytes 1770624 | tf_op jit(solution)/shard_map/convert_element_type | solution.py:425
  39.1 3.5 %fusion.3 = bf16[1728,128]{1,0:T(8,128)(2,1)S(1)} fusion(bf16[128,1152]{1,0:T(8,128)(2,1)} %fusion.12, bf16[1152,1728]{0,1:T(8,128)(2,1)} %param.23), kind=kOutput, calls=%fused_computation.13 | convolution fusion | flops 509829120 | bytes 4718592 | tf_op jit(solution)/shard_map/dot_general | solution.py:195
  42.8 27.0 %all_to_all.39.packed_ref = bf16[8,4,80,128]{3,2,1,0:T(8,128)(2,1)} all-to-all(bf16[8,4,80,128]{3,2,1,0:T(8,128)(2,1)S(1)} %pad_maximum_fusion.1), channel_id=1, replica_groups=mesh['grp'=4,'seq'=8] {'seq'}, dimensions={0} | all-to-all | bytes 1310720 | tf_op jit(solution)/shard_map/all_to_all | solution.py:208
  69.8 7.3 %shard_map.138 = (bf16[8,4,80,128]{3,2,1,0:T(8,128)(2,1)}, bf16[4,80,1024]{2,1,0:T(8,128)(2,1)}) custom-call(bf16[8,4,80,128]{3,2,1,0:T(8,128)(2,1)} %all_to_all.39.packed_ref), custom_call_target="tpu_custom_call" | custom-call | tf_op jit(solution)/shard_map/pallas_call | solution.py:220
  77.1 4.4 %all-to-all-start.2 = ((bf16[8,4,80,128]{3,2,1,0:T(8,128)(2,1)}), bf16[8,4,80,128]{3,2,1,0:T(8,128)(2,1)}, u32[]{:S(2)}, u32[]{:S(2)}) async-start(bf16[8,4,80,128]{3,2,1,0:T(8,128)(2,1)} %get-tuple-element.19), calls=%async_computation.2 | async-start | bytes 1310720 | tf_op jit(solution)/shard_map/all_to_all | solution.py:246
  81.5 1.8 slice.88
  83.3 16.1 %all-to-all-done.2 = bf16[8,4,80,128]{3,2,1,0:T(8,128)(2,1)} async-done(((bf16[8,4,80,128]{3,2,1,0:T(8,128)(2,1)}), bf16[8,4,80,128]{3,2,1,0:T(8,128)(2,1)}, u32[]{:S(2)}, u32[]{:S(2)}) %all-to-all-start.2) | async-done | bytes 655392 | tf_op jit(solution)/shard_map/all_to_all | solution.py:246
  99.4 1.1 slice_bitcast_fusion
  101.4 4.0 %fusion.54 = (f32[128]{0:T(128)S(1)}, f32[128]{0:T(128)S(1)}, f32[128,1152]{1,0:T(8,128)}) fusion(f32[128]{0:T(128)S(1)} %add_rsqrt_fusion, f32[128]{0:T(128)S(1)} %broadcast_multiply_fusion.3, bf16[128,1152]{1,0:T(8,128)(2,1)S(1)} %gather_fusion.2, pred[128]{0:T(512)(128)(4,1)S(1)} %compare_and_fusion, f32[128,3456]{1,0:T(8,128)} %fusion.39, ...), kind=kOutput, calls=%fused_computation.104 | convolution fusion | flops 510934784 | bytes 5900416 | tf_op jit(solution)/shard_map/dot_general | solution.py:439
  105.4 2.6 %scatter_custom_fusion = bf16[128,1152]{1,0:T(8,128)(2,1)} fusion(s32[128]{0:T(128)S(1)} %fusion.49, f32[128,1152]{1,0:T(8,128)} %get-tuple-element.23, f32[128]{0:T(128)S(1)} %get-tuple-element.24, f32[128]{0:T(128)S(1)} %get-tuple-element.25, f32[128]{0:T(128)S(1)} %add_rsqrt_fusion, f32[128]{0:T(128)S(1)} %broadcast_multiply_fusion.3, ...), kind=kCustom, calls=%fused_computation.45 | custom fusion | flops 1622016 | bytes 1477122 | tf_op jit(solution)/shard_map/scatter | solution.py:452
  108.0 4.1 %all-to-all-start.3 = ((bf16[8,16,1152]{2,1,0:T(8,128)(2,1)}), bf16[8,16,1152]{2,1,0:T(8,128)(2,1)}, u32[]{:S(2)}, u32[]{:S(2)}) async-start(bf16[8,16,1152]{2,1,0:T(8,128)(2,1)} %bitcast.24), calls=%async_computation.3 | async-start | bytes 589824 | tf_op jit(solution)/shard_map/all_to_all | solution.py:453
  112.1 1.1 slice_reduce_fusion
  113.2 3.8 %fusion = bf16[1024,1152]{1,0:T(8,128)(2,1)S(1)} fusion(bf16[1024,1280]{1,0:T(8,128)(2,1)} %all-gather.3.cloned.1.call-done, bf16[16]{0:T(256)(128)(2,1)S(1)} %iota_convert_fusion, bf16[1024]{0:T(1024)(128)(2,1)S(1)} %slice_reduce_fusion, f32[16,3456]{1,0:T(8,128)S(1)} %fusion.40), kind=kOutput, calls=%fused_computation.6 | convolution fusion | flops 230047744 | bytes 4794880 | tf_op jit(solution)/shard_map/dot_general | solution.py:214
  117.0 1.5 convolution_convert_fusion.2
  118.6 2.4 %convolution_convert_fusion = bf16[216,1152]{1,0:T(8,128)(2,1)S(1)} fusion(bf16[216,1024]{1,0:T(8,128)(2,1)S(1)} %bitcast.87, bf16[1024,1152]{1,0:T(8,128)(2,1)} %all-gather.5.cloned.1.call-done), kind=kOutput, calls=%fused_computation.7 | convolution fusion | flops 509856768 | bytes 3299328 | tf_op jit(solution)/shard_map/dot_general | solution.py:232
  121.0 0.9 pad_maximum_fusion
  122.5 3.8 %all-to-all-start.4 = ((bf16[4,72,1152]{2,1,0:T(8,128)(2,1)}), bf16[4,72,1152]{2,1,0:T(8,128)(2,1)S(1)}, u32[]{:S(2)}, u32[]{:S(2)}) async-start(bf16[4,72,1152]{2,1,0:T(8,128)(2,1)} %bitcast.29), calls=%async_computation.4 | async-start | bytes 1327104 | tf_op jit(solution)/shard_map/all_to_all | solution.py:238
  126.3 2.6 %fusion.4 = bf16[1,128,1152]{2,1,0:T(8,128)(2,1)} fusion(bf16[576,128]{1,0:T(8,128)(2,1)S(1)} %bitcast.82, bf16[576,1152]{1,0:T(8,128)(2,1)} %param.24, f32[128,3456]{1,0:T(8,128)} %fusion.39, bf16[128,1152]{1,0:T(8,128)(2,1)S(1)} %gather_fusion.2, pred[128]{0:T(512)(128)(4,1)S(1)} %compare_and_fusion), kind=kOutput, calls=%fused_computation.14 | convolution fusion | flops 170606592 | bytes 2654336 | tf_op jit(solution)/shard_map/dot_general | solution.py:435
  128.9 2.2 %scatter_custom_fusion.1 = bf16[128,1152]{1,0:T(8,128)(2,1)} fusion(s32[128]{0:T(128)S(1)} %fusion.48, bf16[128,1152]{1,0:T(8,128)(2,1)} %bitcast.25, bf16[]{:T(256)} %constant.82.clone.1), kind=kCustom, calls=%fused_computation.55 | custom fusion | bytes 295424 | tf_op jit(solution)/shard_map/scatter | solution.py:454
  131.1 4.6 %all-to-all-done.4 = bf16[4,72,1152]{2,1,0:T(8,128)(2,1)S(1)} async-done(((bf16[4,72,1152]{2,1,0:T(8,128)(2,1)}), bf16[4,72,1152]{2,1,0:T(8,128)(2,1)S(1)}, u32[]{:S(2)}, u32[]{:S(2)}) %all-to-all-start.4) | async-done | bytes 663584 | tf_op jit(solution)/shard_map/all_to_all | solution.py:238
  136.5 42.1 %shard_map.139 = bf16[32,72,1152]{2,1,0:T(8,128)(2,1)} custom-call(bf16[72,1152]{1,0:T(8,128)(2,1)} %multiply_convert_fusion.share_ref), custom_call_target="tpu_custom_call" | custom-call | tf_op jit(solution)/shard_map/pallas_call | solution.py:166
  178.6 2.5 %slice.91 = bf16[8,72,1152]{2,1,0:T(8,128)(2,1)} slice(bf16[32,72,1152]{2,1,0:T(8,128)(2,1)} %shard_map.139), slice={[0:8], [0:72], [0:1152]} | slice | bytes 2654208 | tf_op jit(solution)/shard_map/slice | solution.py:245
  181.1 4.4 %slice.89 = bf16[24,72,1152]{2,1,0:T(8,128)(2,1)} slice(bf16[32,72,1152]{2,1,0:T(8,128)(2,1)} %shard_map.139), slice={[8:32], [0:72], [0:1152]} | slice | bytes 7962624 | tf_op jit(solution)/shard_map/slice | solution.py:244
  (67 shorter events, 7.6 us)
Async XLA Ops:
  7.2 11.7 %copy-start = (bf16[1001,1152]{1,0:T(8,128)(2,1)S(1)}, bf16[1001,1152]{1,0:T(8,128)(2,1)}, u32[]{:S(2)}) copy-start(bf16[1001,1152]{1,0:T(8,128)(2,1)} %param.21) | copy-start | bytes 6918916
  7.2 4.4 %copy-start.11 = (s32[1,1,128]{2,1,0:T(1,128)S(1)}, s32[1,1,128]{2,1,0:T(1,128)}, u32[]{:S(2)}) copy-start(s32[1,1,128]{2,1,0:T(1,128)} %param.16) | copy-start | bytes 1540
  7.2 3.4 %copy-start.1 = (bf16[1,128,1152]{2,1,0:T(8,128)(2,1)S(1)}, bf16[1,128,1152]{2,1,0:T(8,128)(2,1)}, u32[]{:S(2)}) copy-start(bf16[1,128,1152]{2,1,0:T(8,128)(2,1)} %param.15) | copy-start | bytes 884740
  7.2 104.9 %all-gather.3.cloned.1.call-start = ((), (), s32[]{:S(2)}) async-start(), calls=%async_computation.5 | async-start | bytes 2949120 | tf_op jit(solution)/shard_map/all_gather | solution.py:399
  8.2 10.6 %copy-start.8 = (s32[1,16]{1,0:T(1,128)S(1)}, s32[1,16]{1,0:T(1,128)}, u32[]{:S(2)}) copy-start(s32[1,16]{1,0:T(1,128)} %param.19) | copy-start | bytes 196
  8.2 10.6 %copy-start.9 = (s32[1,16]{1,0:T(1,128)S(1)}, s32[1,16]{1,0:T(1,128)}, u32[]{:S(2)}) copy-start(s32[1,16]{1,0:T(1,128)} %param.20) | copy-start | bytes 196
  9.9 9.5 %copy-start.7 = (s32[4]{0:T(128)S(1)}, s32[4]{0:T(128)}, u32[]{:S(2)}) copy-start(s32[4]{0:T(128)} %constant.85.clone.1) | copy-start | bytes 52
  9.9 10.2 %copy-start.10 = (s32[1,1,128]{2,1,0:T(1,128)S(1)}, s32[1,1,128]{2,1,0:T(1,128)}, u32[]{:S(2)}) copy-start(s32[1,1,128]{2,1,0:T(1,128)} %param.17) | copy-start | bytes 1540
  12.4 23.1 %all-to-all-start = ((bf16[8,16,1152]{2,1,0:T(8,128)(2,1)}), bf16[8,16,1152]{2,1,0:T(8,128)(2,1)S(1)}, u32[]{:S(2)}, u32[]{:S(2)}) async-start(bf16[8,16,1152]{2,1,0:T(8,128)(2,1)} %bitcast.3), calls=%async_computation | async-start | bytes 589824 | tf_op jit(solution)/shard_map/all_to_all | solution.py:406
  18.7 99.8 %all-gather.5.cloned.1.call-start = ((), (), s32[]{:S(2)}) async-start(), calls=%async_computation.6 | async-start | bytes 2654208 | tf_op jit(solution)/shard_map/all_gather | solution.py:210
  20.2 4.7 %copy-start.6 = (s32[1,128]{1,0:T(1,128)S(1)}, s32[1,128]{1,0:T(1,128)}, u32[]{:S(2)}) copy-start(s32[1,128]{1,0:T(1,128)} %param.18) | copy-start | bytes 1540
  20.2 9.1 %copy-start.2 = (bf16[1,128,1152]{2,1,0:T(8,128)(2,1)S(1)}, bf16[1,128,1152]{2,1,0:T(8,128)(2,1)}, u32[]{:S(2)}) copy-start(bf16[1,128,1152]{2,1,0:T(8,128)(2,1)} %param.25) | copy-start | bytes 884740
  39.1 3.5 %copy-start.4 = (bf16[576,128]{1,0:T(8,128)(2,1)S(1)}, bf16[576,128]{1,0:T(8,128)(2,1)}, u32[]{:S(2)}) copy-start(bf16[576,128]{1,0:T(8,128)(2,1)} %fusion.5) | copy-start | bytes 442372
  77.1 22.4 %all-to-all-start.2 = ((bf16[8,4,80,128]{3,2,1,0:T(8,128)(2,1)}), bf16[8,4,80,128]{3,2,1,0:T(8,128)(2,1)}, u32[]{:S(2)}, u32[]{:S(2)}) async-start(bf16[8,4,80,128]{3,2,1,0:T(8,128)(2,1)} %get-tuple-element.19), calls=%async_computation.2 | async-start | bytes 1310720 | tf_op jit(solution)/shard_map/all_to_all | solution.py:246
  100.5 0.8 copy-start.3
  108.0 14.5 %all-to-all-start.3 = ((bf16[8,16,1152]{2,1,0:T(8,128)(2,1)}), bf16[8,16,1152]{2,1,0:T(8,128)(2,1)}, u32[]{:S(2)}, u32[]{:S(2)}) async-start(bf16[8,16,1152]{2,1,0:T(8,128)(2,1)} %bitcast.24), calls=%async_computation.3 | async-start | bytes 589824 | tf_op jit(solution)/shard_map/all_to_all | solution.py:453
  117.0 1.6 copy-start.5
  121.0 5.2 %slice-start = ((bf16[4,8,72,128]{3,2,0,1:T(8,128)(2,1)}), bf16[1,8,72,128]{3,2,0,1:T(8,128)(2,1)S(1)}, s32[]{:S(2)}) async-start(bf16[4,8,72,128]{3,2,0,1:T(8,128)(2,1)} %copy-done.3), calls=%async_computation.7 | async-start | bytes 294912 | tf_op jit(solution)/shard_map/slice | solution.py:248
  122.5 13.3 %all-to-all-start.4 = ((bf16[4,72,1152]{2,1,0:T(8,128)(2,1)}), bf16[4,72,1152]{2,1,0:T(8,128)(2,1)S(1)}, u32[]{:S(2)}, u32[]{:S(2)}) async-start(bf16[4,72,1152]{2,1,0:T(8,128)(2,1)} %bitcast.29), calls=%async_computation.4 | async-start | bytes 1327104 | tf_op jit(solution)/shard_map/all_to_all | solution.py:238
Sparse Core Ops, SparseCore 0:
  10.1 41.6 all-gather.2
  53.9 31.9 all-gather.4
